TPU v7x, 32 devices: a whole 2x2x4 slice. The times are simulated.
32 devices in a mesh: row: 4 (over z), col: 4 (over y, x), pupil: 2 (over core).
Axes of the slice: x: 2, y: 2, z: 4, core: 2. Of those that a mesh axis runs over, the one named last changes fastest.
Arguments:
- phase: float32 [512, 8192], P('row', 'col'), may hold values from -3.140625 to 3.140625
- band_offsets: int32 [2, 2], P('pupil'), may hold values from 0 to 8191
- depth_codes: int32 [8], replicated, may hold values from -6 to 6
Outputs:
- retina: float32 [8, 512, 512], P('pupil', ('row', 'col'))
Inputs may be any that keep to these rules, and one draw needn't show every extreme that they name: `band_offsets`: A band wraps around modulo 8192.
All inputs are finite; a program needn't handle non-finite values.
Results may differ from a plain program's by a relative error of at most 0.0016.
Values sent between devices are 32-bit elements; how exact they have to be, the bound alone decides.
No kernel may reach another device: no remote copies, remote signals or barrier semaphores. Data moves between devices by JAX's collectives and lax.ppermute only.
A program may use at most 64 MiB of HBM per device.

v0:
```python
import functools
import math

import jax
import jax.numpy as jnp
from jax import lax
from jax.experimental import pallas as pl
from jax.experimental.pallas import tpu as pltpu
from jax.sharding import PartitionSpec as P

HOLO = 8192
BAND = 512
LANES = 512
STEP = 16
F32 = jnp.float32
BF16 = jnp.bfloat16
I32 = jnp.int32


def turn_parts(r, q):
    z = r * r
    s = ((-1.9515295891e-4 * z + 8.3321608736e-3) * z - 1.6666654611e-1) * z * r + r
    c = ((2.443315711809948e-5 * z - 1.388731625493765e-3) * z + 4.166664568298827e-2) * (z * z) - 0.5 * z + 1.0
    odd = (q & 1) == 1
    cs = jnp.where(odd, s, c)
    sn = jnp.where(odd, c, s)
    return jnp.where(((q + 1) & 2) == 2, -cs, cs), jnp.where((q & 2) == 2, -sn, sn)


def circle(k, size):
    quarter = size // 4
    k = k + quarter // 2
    q = k >> (quarter.bit_length() - 1)
    r = (k & (quarter - 1)) - quarter // 2
    return turn_parts(r.astype(F32) * (2.0 * math.pi / size), q)


def radians(x):
    qf = jnp.floor(x * (2.0 / math.pi) + 0.5)
    r = ((x - qf * 1.5703125) - qf * 4.837512969970703125e-4) - qf * 7.54978995489188216e-8
    return turn_parts(r, qf.astype(I32))


def split(x):
    hi = x.astype(BF16)
    return hi, (x - hi.astype(F32)).astype(BF16)


def mm(a, b, nt=False):
    dims = (((1,), (1 if nt else 0,)), ((), ()))
    return lax.dot_general(a, b, dims, preferred_element_type=F32)


def mm3(ah, al, bh, bl, nt=False):
    return mm(ah, bh, nt) + (mm(al, bh, nt) + mm(ah, bl, nt))


def half_kernel(n_col, offs, ph, *refs):
    outs = refs[:n_col]
    field, table, a_re, a_im, b_re, b_im = refs[n_col:]
    rows, cols = ph.shape
    share = BAND // n_col
    offset, me = offs[0, 1], lax.axis_index("col")
    n0 = me * cols
    per = share // STEP

    def fill(i, _):
        at = pl.multiple_of(i * STEP, STEP)
        for j in range(0, cols, LANES):
            c, s = radians(ph[pl.ds(at, STEP), j : j + LANES])
            field[pl.ds(at, STEP), j : j + LANES] = c.astype(BF16)
            field[pl.ds(rows + at, STEP), j : j + LANES] = s.astype(BF16)
        return 0

    lax.fori_loop(0, rows // STEP, fill, 0)
    for j in range(0, cols, LANES):
        n = n0 + j + lax.broadcasted_iota(I32, (STEP, LANES), 1)
        low = lax.broadcasted_iota(I32, (STEP, LANES), 0)
        c, s = circle((low * n) & (HOLO - 1), HOLO)
        b_re[:, j : j + LANES] = c
        b_im[:, j : j + LANES] = -s
        n = n0 + j + lax.broadcasted_iota(I32, (n_col * per, LANES), 1)
        row = lax.broadcasted_iota(I32, (n_col * per, LANES), 0)
        block = me ^ (row // per)
        v = block * share + (row % per) * STEP
        c, s = circle((((offset + v) & (HOLO - 1)) * n) & (HOLO - 1), HOLO)
        a_re[:, j : j + LANES] = c
        a_im[:, j : j + LANES] = -s
    for t in list(range(1, n_col)) + [0]:
        buf = table.at[t % 2]
        for j in range(0, cols, LANES):
            br = b_re[:, j : j + LANES]
            bi = b_im[:, j : j + LANES]
            for h in range(per):
                ar = a_re[t * per + h : t * per + h + 1, j : j + LANES]
                ai = a_im[t * per + h : t * per + h + 1, j : j + LANES]
                buf[h * STEP : (h + 1) * STEP, j : j + LANES] = (ar * br - ai * bi).astype(BF16)
                buf[share + h * STEP : share + (h + 1) * STEP, j : j + LANES] = (ar * bi + ai * br).astype(BF16)
        prod = mm(buf[...], field[...], nt=True)
        outs[t][:share, :] = prod[:share, :rows] - prod[share:, rows:]
        outs[t][share:, :] = prod[:share, rows:] + prod[share:, :rows]


def rows_kernel(n_row, n_col, n_pupil, depths, spacing, offs, codes, fl_hi, fl_lo, lens_hi, lens_lo, ev):
    offset = offs[0, 0]
    r, c, p = (lax.axis_index(a) for a in ("row", "col", "pupil"))
    own = depths // n_pupil
    code = [codes[((d // own) ^ p) * own + d % own] for d in range(depths)]
    rows_here = fl_hi.shape[0] // n_row
    xs = BAND // (n_row * n_col)
    share = BAND // n_col
    big = 4 * (BAND // 2) ** 2
    chunk = 32

    def fill(i, _):
        at = pl.multiple_of(i * chunk, chunk)
        row = at + lax.broadcasted_iota(I32, (chunk, BAND), 0)
        u = lax.broadcasted_iota(I32, (chunk, BAND), 1)
        m = (r ^ (row // rows_here)) * rows_here + row % rows_here
        k = (((offset + u) & (HOLO - 1)) * ((m * spacing) & (HOLO - 1))) & (HOLO - 1)
        cs, sn = circle(k, HOLO)
        hi, lo = split(cs)
        fl_hi[pl.ds(at, chunk), :BAND] = hi
        fl_lo[pl.ds(at, chunk), :BAND] = lo
        hi, lo = split(-sn)
        fl_hi[pl.ds(at, chunk), BAND:] = hi
        fl_lo[pl.ds(at, chunk), BAND:] = lo
        return 0

    lax.fori_loop(0, n_row * rows_here // chunk, fill, 0)

    scale = 1.0 / math.sqrt(BAND)
    u = lax.broadcasted_iota(I32, (1, BAND), 1) - BAND // 2
    v = c * share + lax.broadcasted_iota(I32, (1, share), 1) - BAND // 2
    for t in range(n_col):
        x = (r * n_col + (c ^ t)) * xs + lax.broadcasted_iota(I32, (xs, BAND), 0)
        uu = lax.broadcasted_iota(I32, (xs, BAND), 1)
        g_re, g_im = circle((x * uu) & (BAND - 1), BAND)
        g_re = g_re * scale
        g_im = g_im * scale
        for d in range(depths):
            e_re, e_im = circle((code[d] * (u * u)) & (big - 1), big)
            re = g_re * e_re - g_im * e_im
            im = g_re * e_im + g_im * e_re
            at = (t * depths + d) * xs
            hi, lo = split(re)
            lens_hi[at : at + xs, :BAND] = hi
            lens_lo[at : at + xs, :BAND] = lo
            hi, lo = split(im)
            lens_hi[at : at + xs, BAND:] = hi
            lens_lo[at : at + xs, BAND:] = lo
    for d in range(depths):
        e_re, e_im = circle((code[d] * (v * v)) & (big - 1), big)
        ev[d : d + 1, :share] = e_re
        ev[d : d + 1, share:] = e_im


def image_table_kernel(n_col, g_hi, g_lo):
    c = lax.axis_index("col")
    share = BAND // n_col
    chunk = 32
    scale = 1.0 / math.sqrt(BAND)

    def fill(i, _):
        at = pl.multiple_of(i * chunk, chunk)
        row = at + lax.broadcasted_iota(I32, (chunk, BAND), 0)
        y = lax.broadcasted_iota(I32, (chunk, BAND), 1)
        v = (c ^ (row // share)) * share + row % share
        cs, sn = circle((v * y) & (BAND - 1), BAND)
        hi, lo = split(cs * scale)
        g_hi[pl.ds(at, chunk), :BAND] = hi
        g_lo[pl.ds(at, chunk), :BAND] = lo
        hi, lo = split(sn * scale)
        g_hi[pl.ds(at, chunk), BAND:] = hi
        g_lo[pl.ds(at, chunk), BAND:] = lo
        return 0

    lax.fori_loop(0, BAND // chunk, fill, 0)


def lens_kernel(n_row, n_col, depths, *refs):
    halves = refs[:n_row]
    fl_hi, fl_lo, lens_hi, lens_lo, ev = refs[n_row : n_row + 5]
    outs = refs[n_row + 5 : n_row + 5 + n_col]
    w_hi, w_lo = refs[n_row + 5 + n_col :]
    share = BAND // n_col
    xs = BAND // (n_row * n_col)
    x = jnp.concatenate([h[...] for h in halves], axis=1)
    hi, lo = split(x)
    s = mm3(hi, lo, fl_hi[...], fl_lo[...])
    s_re = (s[:share, :BAND] - s[share:, BAND:]) * (1.0 / HOLO)
    s_im = (s[:share, BAND:] + s[share:, :BAND]) * (1.0 / HOLO)
    hi, lo = split(s_re)
    w_hi[:share, :BAND] = hi
    w_lo[:share, :BAND] = lo
    w_hi[share:, BAND:] = hi
    w_lo[share:, BAND:] = lo
    hi, lo = split(s_im)
    w_hi[share:, :BAND] = hi
    w_lo[share:, :BAND] = lo
    w_hi[:share, BAND:] = -hi
    w_lo[:share, BAND:] = -lo
    block = depths * xs
    for t in list(range(1, n_col)) + [0]:
        at = t * block
        z = mm3(lens_hi[at : at + block, :], lens_lo[at : at + block, :], w_hi[...], w_lo[...], nt=True)
        for d in range(depths):
            re = z[d * xs : (d + 1) * xs, :share]
            im = z[d * xs : (d + 1) * xs, share:]
            e_re = ev[d : d + 1, :share]
            e_im = ev[d : d + 1, share:]
            outs[t][d * xs : (d + 1) * xs, :] = re * e_re - im * e_im
            outs[t][block + d * xs : block + (d + 1) * xs, :] = re * e_im + im * e_re


def image_kernel(n_col, n_pupil, *refs):
    blocks = refs[:n_col]
    g_hi, g_lo = refs[n_col : n_col + 2]
    outs = refs[n_col + 2 :]
    x = jnp.concatenate([b[...] for b in blocks], axis=1)
    hi, lo = split(x)
    z = mm3(hi, lo, g_hi[...], g_lo[...])
    n = x.shape[0] // 2
    re = z[:n, :BAND] - z[n:, BAND:]
    im = z[:n, BAND:] + z[n:, :BAND]
    power = re * re + im * im
    m = n // n_pupil
    for t in range(n_pupil):
        outs[t][...] = power[t * m : (t + 1) * m]


def spec(shape, dtype=F32):
    return jax.ShapeDtypeStruct(shape, dtype)


def call(kernel, outs, smem, scratch=(), n_in=0):
    vm = pl.BlockSpec(memory_space=pltpu.VMEM)
    return pl.pallas_call(
        kernel,
        out_shape=outs,
        in_specs=[pl.BlockSpec(memory_space=pltpu.SMEM)] * smem + [vm] * n_in,
        out_specs=[vm] * len(outs),
        scratch_shapes=list(scratch),
        compiler_params=pltpu.CompilerParams(vmem_limit_bytes=48 * 1024 * 1024),
    )


def swap(x, axis, t):
    n = lax.axis_size(axis)
    return lax.ppermute(x, axis, [(i, i ^ t) for i in range(n)])


def local(phase, band_offsets, depth_codes):
    rows, cols = phase.shape
    n_row, n_col, n_pupil = (lax.axis_size(a) for a in ("row", "col", "pupil"))
    depths = depth_codes.shape[0]
    own = depths // n_pupil
    share = BAND // n_col
    xs = BAND // (n_row * n_col)
    block = depths * xs
    spacing = HOLO // (rows * n_row)

    part = call(
        functools.partial(half_kernel, n_col),
        [spec((2 * share, rows))] * n_col,
        1,
        [
            pltpu.VMEM((2 * rows, cols), BF16),
            pltpu.VMEM((2, 2 * share, cols), BF16),
            pltpu.VMEM((BAND // STEP, cols), F32),
            pltpu.VMEM((BAND // STEP, cols), F32),
            pltpu.VMEM((STEP, cols), F32),
            pltpu.VMEM((STEP, cols), F32),
        ],
        1,
    )(band_offsets, phase)
    got = [swap(part[t], "col", t) for t in range(n_col - 1, 0, -1)]

    fl_hi, fl_lo, lens_hi, lens_lo, ev = call(
        functools.partial(rows_kernel, n_row, n_col, n_pupil, depths, spacing),
        [
            spec((n_row * rows, 2 * BAND), BF16),
            spec((n_row * rows, 2 * BAND), BF16),
            spec((n_col * block, 2 * BAND), BF16),
            spec((n_col * block, 2 * BAND), BF16),
            spec((depths, 2 * share)),
        ],
        2,
    )(band_offsets, depth_codes)
    g_hi, g_lo = call(
        functools.partial(image_table_kernel, n_col),
        [spec((BAND, 2 * BAND), BF16)] * 2,
        0,
    )()

    half = part[0]
    for h in got:
        half = half + h
    halves = [half] + [swap(half, "row", t) for t in range(1, n_row)]
    lens = call(
        functools.partial(lens_kernel, n_row, n_col, depths),
        [spec((2 * block, share))] * n_col,
        0,
        [pltpu.VMEM((2 * share, 2 * BAND), BF16)] * 2,
        n_row + 5,
    )(*halves, fl_hi, fl_lo, lens_hi, lens_lo, ev)
    blocks = [lens[0]] + [swap(lens[t], "col", t) for t in range(n_col - 1, 0, -1)][::-1]
    power = call(
        functools.partial(image_kernel, n_col, n_pupil),
        [spec((block // n_pupil, BAND))] * n_pupil,
        0,
        (),
        n_col + 2,
    )(*blocks, g_hi, g_lo)
    total = power[0]
    for t in range(1, n_pupil):
        total = total + swap(power[t], "pupil", t)
    total = total * (1.0 / (band_offsets.shape[0] * n_pupil))
    return total.reshape(own, xs, BAND)


def solution(mesh):
    in_specs = (P("row", "col"), P("pupil", None), P())
    out_specs = P("pupil", ("row", "col"), None)
    return jax.shard_map(local, mesh=mesh, in_specs=in_specs, out_specs=out_specs, check_vma=False)
```

profile of v0, /device:TPU:17, one launch (start us, length us, event | category | flops | bytes accessed | tf_op | source)
XLA Modules:
  0.0 53.1 jit_solution(14988925450633338639)
XLA Ops:
  0.0 0.0 copy-start
  0.0 1.2 %copy-done = f32[128,2048]{1,0:T(8,128)S(1)} copy-done((f32[128,2048]{1,0:T(8,128)S(1)}, f32[128,2048]{1,0:T(8,128)}, u32[]{:S(2)}) %copy-start) | copy-done | bytes 1048600
  1.2 0.0 copy-start.1
  1.2 0.7 %copy-done.1 = s32[1,2]{1,0:T(1,128)S(1)} copy-done((s32[1,2]{1,0:T(1,128)S(1)}, s32[1,2]{1,0:T(1,128)}, u32[]{:S(2)}) %copy-start.1) | copy-done | bytes 32
  1.9 4.0 %shard_map.37 = (f32[256,128]{1,0:T(8,128)S(1)}, f32[256,128]{1,0:T(8,128)S(1)}, f32[256,128]{1,0:T(8,128)S(1)}, f32[256,128]{1,0:T(8,128)S(1)}) custom-call(s32[1,2]{1,0:T(1,128)S(1)} %copy-done.1, f32[128,2048]{1,0:T(8,128)S(1)} %copy-done), custom_call_target="tpu_custom_call" | custom-call | tf_op jit(solution)/shard_map/pallas_call | solution.py:263
  5.9 2.2 %collective-permute-start = (f32[256,128]{1,0:T(8,128)S(1)}, f32[256,128]{1,0:T(8,128)S(1)}, u32[]{:S(2)}, u32[]{:S(2)}) collective-permute-start(f32[256,128]{1,0:T(8,128)S(1)} %get-tuple-element.23), channel_id=1, source_target_pairs={{0,6},{2,4},{4,2},{6,0},{1,7},{3,5},{5,3},{7,1},{8,14},{10,12},{12... | collective-permute-start | bytes 393224 | tf_op jit(solution)/shard_map/ppermute | solution.py:250
  8.1 0.2 collective-permute-start.1
  8.4 0.3 collective-permute-start.2
  8.6 2.6 %collective-permute-done = f32[256,128]{1,0:T(8,128)S(1)} collective-permute-done((f32[256,128]{1,0:T(8,128)S(1)}, f32[256,128]{1,0:T(8,128)S(1)}, u32[]{:S(2)}, u32[]{:S(2)}) %collective-permute-start) | collective-permute-done | bytes 131104 | tf_op jit(solution)/shard_map/ppermute | solution.py:250
  11.3 3.8 %collective-permute-done.1 = f32[256,128]{1,0:T(8,128)S(1)} collective-permute-done((f32[256,128]{1,0:T(8,128)S(1)}, f32[256,128]{1,0:T(8,128)S(1)}, u32[]{:S(2)}, u32[]{:S(2)}) %collective-permute-start.1) | collective-permute-done | bytes 131104 | tf_op jit(solution)/shard_map/ppermute | solution.py:250
  15.1 0.0 collective-permute-done.2
  15.1 1.3 %collective-permute-start.3 = (f32[256,128]{1,0:T(8,128)S(1)}, f32[256,128]{1,0:T(8,128)S(1)}, u32[]{:S(2)}, u32[]{:S(2)}) collective-permute-start(f32[256,128]{1,0:T(8,128)S(1)} %add_add_fusion.refs_0_), channel_id=1, source_target_pairs={{0,8},{8,0},{16,24},{24,16},{1,9},{9,1},{17,25},{25,17},{2,10},{10... | collective-permute-start | bytes 393224 | tf_op jit(solution)/shard_map/ppermute | solution.py:250
  16.5 0.1 collective-permute-start.4
  16.5 1.3 %collective-permute-start.5 = (f32[256,128]{1,0:T(8,128)S(1)}, f32[256,128]{1,0:T(8,128)S(1)}, u32[]{:S(2)}, u32[]{:S(2)}) collective-permute-start(f32[256,128]{1,0:T(8,128)S(1)} %add_add_fusion.refs_0_), channel_id=1, source_target_pairs={{0,24},{8,16},{16,8},{24,0},{1,25},{9,17},{17,9},{25,1},{2,26},{10... | collective-permute-start | bytes 393224 | tf_op jit(solution)/shard_map/ppermute | solution.py:250
  17.8 0.0 copy-start.2
  17.8 0.7 %copy-done.2 = s32[8]{0:T(128)S(1)} copy-done((s32[8]{0:T(128)S(1)}, s32[8]{0:T(128)}, u32[]{:S(2)}) %copy-start.2) | copy-done | bytes 56
  18.5 5.6 %shard_map.38 = (bf16[512,1024]{1,0:T(8,128)(2,1)S(1)}, bf16[512,1024]{1,0:T(8,128)(2,1)S(1)}, bf16[1024,1024]{1,0:T(8,128)(2,1)S(1)}, bf16[1024,1024]{1,0:T(8,128)(2,1)}, f32[8,256]{1,0:T(8,128)S(1)}) custom-call(s32[1,2]{1,0:T(1,128)S(1)} %copy-done.1, s32[8]{0:T(128)S(1)} %copy-done.2), custom_call_target="tpu_custom_call" | custom-call | tf_op jit(solution)/shard_map/pallas_call | solution.py:279
  24.1 0.0 collective-permute-done.3.refs_1_
  24.1 0.0 collective-permute-done.4.refs_2_
  24.1 5.1 %collective-permute-done.5.refs_3_ = f32[256,128]{1,0:T(8,128)S(1)} collective-permute-done((f32[256,128]{1,0:T(8,128)S(1)}, f32[256,128]{1,0:T(8,128)S(1)}, u32[]{:S(2)}, u32[]{:S(2)}) %collective-permute-start.5) | collective-permute-done | bytes 131104 | tf_op jit(solution)/shard_map/ppermute | solution.py:250
  29.2 4.4 %shard_map.39 = (f32[512,128]{1,0:T(8,128)S(1)}, f32[512,128]{1,0:T(8,128)S(1)}, f32[512,128]{1,0:T(8,128)S(1)}, f32[512,128]{1,0:T(8,128)S(1)}) custom-call(f32[256,128]{1,0:T(8,128)S(1)} %add_add_fusion.refs_0_, f32[256,128]{1,0:T(8,128)S(1)} %collective-permute-done.3.refs_1_, f32[256,128]{1,0:T(8,128)S(1)} %collective-permute-done.4.refs_2_, ...), custom_call_target="tpu_custom_call" | custom-call | tf_op jit(solution)/shard_map/pallas_call | solution.py:300
  33.7 1.3 %collective-permute-start.6 = (f32[512,128]{1,0:T(8,128)S(1)}, f32[512,128]{1,0:T(8,128)S(1)}, u32[]{:S(2)}, u32[]{:S(2)}) collective-permute-start(f32[512,128]{1,0:T(8,128)S(1)} %get-tuple-element.32), channel_id=1, source_target_pairs={{0,2},{2,0},{4,6},{6,4},{1,3},{3,1},{5,7},{7,5},{8,10},{10,8},{12,... | collective-permute-start | bytes 786440 | tf_op jit(solution)/shard_map/ppermute | solution.py:250
  34.9 0.2 collective-permute-start.7
  35.1 1.3 %collective-permute-start.8 = (f32[512,128]{1,0:T(8,128)S(1)}, f32[512,128]{1,0:T(8,128)S(1)}, u32[]{:S(2)}, u32[]{:S(2)}) collective-permute-start(f32[512,128]{1,0:T(8,128)S(1)} %get-tuple-element.34), channel_id=1, source_target_pairs={{0,6},{2,4},{4,2},{6,0},{1,7},{3,5},{5,3},{7,1},{8,14},{10,12},{12... | collective-permute-start | bytes 786440 | tf_op jit(solution)/shard_map/ppermute | solution.py:250
  36.4 2.0 %shard_map.40 = (bf16[512,1024]{1,0:T(8,128)(2,1)S(1)}, bf16[512,1024]{1,0:T(8,128)(2,1)S(1)}) custom-call(), custom_call_target="tpu_custom_call" | custom-call | tf_op jit(solution)/shard_map/pallas_call | solution.py:290
  38.4 1.7 %collective-permute-done.6.refs_1_ = f32[512,128]{1,0:T(8,128)S(1)} collective-permute-done((f32[512,128]{1,0:T(8,128)S(1)}, f32[512,128]{1,0:T(8,128)S(1)}, u32[]{:S(2)}, u32[]{:S(2)}) %collective-permute-start.6) | collective-permute-done | bytes 262176 | tf_op jit(solution)/shard_map/ppermute | solution.py:250
  40.1 0.9 %collective-permute-done.7.refs_2_ = f32[512,128]{1,0:T(8,128)S(1)} collective-permute-done((f32[512,128]{1,0:T(8,128)S(1)}, f32[512,128]{1,0:T(8,128)S(1)}, u32[]{:S(2)}, u32[]{:S(2)}) %collective-permute-start.7) | collective-permute-done | bytes 262176 | tf_op jit(solution)/shard_map/ppermute | solution.py:250
  41.0 5.8 %collective-permute-done.8.refs_3_ = f32[512,128]{1,0:T(8,128)S(1)} collective-permute-done((f32[512,128]{1,0:T(8,128)S(1)}, f32[512,128]{1,0:T(8,128)S(1)}, u32[]{:S(2)}, u32[]{:S(2)}) %collective-permute-start.8) | collective-permute-done | bytes 262176 | tf_op jit(solution)/shard_map/ppermute | solution.py:250
  46.8 1.8 %shard_map.41 = (f32[128,512]{1,0:T(8,128)S(1)}, f32[128,512]{1,0:T(8,128)S(1)}) custom-call(f32[512,128]{1,0:T(8,128)S(1)} %get-tuple-element.31.refs_0_, f32[512,128]{1,0:T(8,128)S(1)} %collective-permute-done.6.refs_1_, f32[512,128]{1,0:T(8,128)S(1)} %collective-permute-done.7.refs_2_, f32[512,128]{1,0:T(8,128)S(1)} %collective-permute-done.8.refs_3_, ...), custom_call_target="tpu_custom_call" | custom-call | tf_op jit(solution)/shard_map/pallas_call | solution.py:308
  48.6 2.5 %collective-permute-start.9 = (f32[128,512]{1,0:T(8,128)S(1)}, f32[128,512]{1,0:T(8,128)S(1)}, u32[]{:S(2)}, u32[]{:S(2)}) collective-permute-start(f32[128,512]{1,0:T(8,128)S(1)} %get-tuple-element.38), channel_id=1, source_target_pairs={{0,1},{1,0},{2,3},{3,2},{4,5},{5,4},{6,7},{7,6},{8,9},{9,8},{10,11... | collective-permute-start | bytes 786440 | tf_op jit(solution)/shard_map/ppermute | solution.py:250
  51.1 1.2 %collective-permute-done.9 = f32[128,512]{1,0:T(8,128)S(1)} collective-permute-done((f32[128,512]{1,0:T(8,128)S(1)}, f32[128,512]{1,0:T(8,128)S(1)}, u32[]{:S(2)}, u32[]{:S(2)}) %collective-permute-start.9) | collective-permute-done | bytes 262176 | tf_op jit(solution)/shard_map/ppermute | solution.py:250
  52.3 0.8 %add_multiply_fusion = f32[128,512]{1,0:T(8,128)} fusion(f32[128,512]{1,0:T(8,128)S(1)} %get-tuple-element.37, f32[128,512]{1,0:T(8,128)S(1)} %collective-permute-done.9), kind=kLoop, calls=%fused_computation | loop fusion | flops 131072 | bytes 786432 | tf_op jit(solution)/shard_map/mul | solution.py:318
  (1 shorter events, 0.0 us)
Async XLA Ops:
  0.0 1.2 %copy-start = (f32[128,2048]{1,0:T(8,128)S(1)}, f32[128,2048]{1,0:T(8,128)}, u32[]{:S(2)}) copy-start(f32[128,2048]{1,0:T(8,128)} %ph.1) | copy-start | bytes 3145732
  1.2 0.7 %copy-start.1 = (s32[1,2]{1,0:T(1,128)S(1)}, s32[1,2]{1,0:T(1,128)}, u32[]{:S(2)}) copy-start(s32[1,2]{1,0:T(1,128)} %offs.3) | copy-start | bytes 28
  5.9 5.3 %collective-permute-start = (f32[256,128]{1,0:T(8,128)S(1)}, f32[256,128]{1,0:T(8,128)S(1)}, u32[]{:S(2)}, u32[]{:S(2)}) collective-permute-start(f32[256,128]{1,0:T(8,128)S(1)} %get-tuple-element.23), channel_id=1, source_target_pairs={{0,6},{2,4},{4,2},{6,0},{1,7},{3,5},{5,3},{7,1},{8,14},{10,12},{12... | collective-permute-start | bytes 393224 | tf_op jit(solution)/shard_map/ppermute | solution.py:250
  8.1 6.9 %collective-permute-start.1 = (f32[256,128]{1,0:T(8,128)S(1)}, f32[256,128]{1,0:T(8,128)S(1)}, u32[]{:S(2)}, u32[]{:S(2)}) collective-permute-start(f32[256,128]{1,0:T(8,128)S(1)} %get-tuple-element.24), channel_id=1, source_target_pairs={{0,4},{2,6},{4,0},{6,2},{1,5},{3,7},{5,1},{7,3},{8,12},{10,14},{12... | collective-permute-start | bytes 393224 | tf_op jit(solution)/shard_map/ppermute | solution.py:250
  8.4 6.7 %collective-permute-start.2 = (f32[256,128]{1,0:T(8,128)S(1)}, f32[256,128]{1,0:T(8,128)S(1)}, u32[]{:S(2)}, u32[]{:S(2)}) collective-permute-start(f32[256,128]{1,0:T(8,128)S(1)} %get-tuple-element.25), channel_id=1, source_target_pairs={{0,2},{2,0},{4,6},{6,4},{1,3},{3,1},{5,7},{7,5},{8,10},{10,8},{12,... | collective-permute-start | bytes 393224 | tf_op jit(solution)/shard_map/ppermute | solution.py:250
  15.1 9.0 %collective-permute-start.3 = (f32[256,128]{1,0:T(8,128)S(1)}, f32[256,128]{1,0:T(8,128)S(1)}, u32[]{:S(2)}, u32[]{:S(2)}) collective-permute-start(f32[256,128]{1,0:T(8,128)S(1)} %add_add_fusion.refs_0_), channel_id=1, source_target_pairs={{0,8},{8,0},{16,24},{24,16},{1,9},{9,1},{17,25},{25,17},{2,10},{10... | collective-permute-start | bytes 393224 | tf_op jit(solution)/shard_map/ppermute | solution.py:250
  16.5 7.6 %collective-permute-start.4 = (f32[256,128]{1,0:T(8,128)S(1)}, f32[256,128]{1,0:T(8,128)S(1)}, u32[]{:S(2)}, u32[]{:S(2)}) collective-permute-start(f32[256,128]{1,0:T(8,128)S(1)} %add_add_fusion.refs_0_), channel_id=1, source_target_pairs={{0,16},{8,24},{16,0},{24,8},{1,17},{9,25},{17,1},{25,9},{2,18},{10... | collective-permute-start | bytes 393224 | tf_op jit(solution)/shard_map/ppermute | solution.py:250
  16.5 12.7 %collective-permute-start.5 = (f32[256,128]{1,0:T(8,128)S(1)}, f32[256,128]{1,0:T(8,128)S(1)}, u32[]{:S(2)}, u32[]{:S(2)}) collective-permute-start(f32[256,128]{1,0:T(8,128)S(1)} %add_add_fusion.refs_0_), channel_id=1, source_target_pairs={{0,24},{8,16},{16,8},{24,0},{1,25},{9,17},{17,9},{25,1},{2,26},{10... | collective-permute-start | bytes 393224 | tf_op jit(solution)/shard_map/ppermute | solution.py:250
  17.8 0.7 %copy-start.2 = (s32[8]{0:T(128)S(1)}, s32[8]{0:T(128)}, u32[]{:S(2)}) copy-start(s32[8]{0:T(128)} %codes.1) | copy-start | bytes 100
  33.7 6.4 %collective-permute-start.6 = (f32[512,128]{1,0:T(8,128)S(1)}, f32[512,128]{1,0:T(8,128)S(1)}, u32[]{:S(2)}, u32[]{:S(2)}) collective-permute-start(f32[512,128]{1,0:T(8,128)S(1)} %get-tuple-element.32), channel_id=1, source_target_pairs={{0,2},{2,0},{4,6},{6,4},{1,3},{3,1},{5,7},{7,5},{8,10},{10,8},{12,... | collective-permute-start | bytes 786440 | tf_op jit(solution)/shard_map/ppermute | solution.py:250
  34.9 6.0 %collective-permute-start.7 = (f32[512,128]{1,0:T(8,128)S(1)}, f32[512,128]{1,0:T(8,128)S(1)}, u32[]{:S(2)}, u32[]{:S(2)}) collective-permute-start(f32[512,128]{1,0:T(8,128)S(1)} %get-tuple-element.33), channel_id=1, source_target_pairs={{0,4},{2,6},{4,0},{6,2},{1,5},{3,7},{5,1},{7,3},{8,12},{10,14},{12... | collective-permute-start | bytes 786440 | tf_op jit(solution)/shard_map/ppermute | solution.py:250
  35.1 11.7 %collective-permute-start.8 = (f32[512,128]{1,0:T(8,128)S(1)}, f32[512,128]{1,0:T(8,128)S(1)}, u32[]{:S(2)}, u32[]{:S(2)}) collective-permute-start(f32[512,128]{1,0:T(8,128)S(1)} %get-tuple-element.34), channel_id=1, source_target_pairs={{0,6},{2,4},{4,2},{6,0},{1,7},{3,5},{5,3},{7,1},{8,14},{10,12},{12... | collective-permute-start | bytes 786440 | tf_op jit(solution)/shard_map/ppermute | solution.py:250
  48.6 3.7 %collective-permute-start.9 = (f32[128,512]{1,0:T(8,128)S(1)}, f32[128,512]{1,0:T(8,128)S(1)}, u32[]{:S(2)}, u32[]{:S(2)}) collective-permute-start(f32[128,512]{1,0:T(8,128)S(1)} %get-tuple-element.38), channel_id=1, source_target_pairs={{0,1},{1,0},{2,3},{3,2},{4,5},{5,4},{6,7},{7,6},{8,9},{9,8},{10,11... | collective-permute-start | bytes 786440 | tf_op jit(solution)/shard_map/ppermute | solution.py:250
where the time goes:
time: 53.3 us; the launch traced here: 53.1 us
  waiting for transfers between devices  21.1 us (40%)
  Pallas kernels  17.9 us (34%)
  starting transfers between devices  10.7 us (20%)
  local copies, waits for them, and re-layouts  2.53 us (5%)
  other arithmetic  0.78 us (1%)
    ppermute x10, waiting for transfers between devices, swap(): return lax.ppermute(x, axis, [(i, i ^ t) for i in range(n)])  21.1 us
    ppermute x10, starting transfers between devices, swap(): return lax.ppermute(x, axis, [(i, i ^ t) for i in range(n)])  10.7 us
    pallas_call x1, Pallas kernels, local(): call(functools.partial(rows_kernel, n_row, n_col, n_pupil, depths, spacin...  5.61 us
    pallas_call x1, Pallas kernels, local(): call(functools.partial(lens_kernel, n_row, n_col, depths), [spec((2 * blo...  4.42 us
    pallas_call x1, Pallas kernels, local(): call(functools.partial(half_kernel, n_col), [spec((2 * share, rows))] * n...  4.02 us
    unnamed x6, local copies, waits for them, and re-layouts  2.53 us
    pallas_call x1, Pallas kernels, local(): call(functools.partial(image_table_kernel, n_col), [spec((BAND, 2 * BAND)...  2.03 us
    pallas_call x1, Pallas kernels, local(): call(functools.partial(image_kernel, n_col, n_pupil), [spec((block // n_p...  1.81 us
  transfers between devices with their start and end apart: 10, of which 7 were waited for; matrix products, arithmetic and copies ran while one was open for 0% of the time, Pallas kernels for 14%

commit v1 on v0

v1 whole, which is shorter than its diff:
```python
import functools
import math

import jax
import jax.numpy as jnp
from jax import lax
from jax.experimental import pallas as pl
from jax.experimental.pallas import tpu as pltpu
from jax.sharding import PartitionSpec as P


HOLO = 8192
BAND = 512
LANES = 512
STEP = 16
CHUNKS = 2
F32 = jnp.float32
BF16 = jnp.bfloat16
I32 = jnp.int32


def turn_parts(r, q):
    z = r * r
    s = ((-1.9515295891e-4 * z + 8.3321608736e-3) * z - 1.6666654611e-1) * z * r + r
    c = ((2.443315711809948e-5 * z - 1.388731625493765e-3) * z + 4.166664568298827e-2) * (z * z) - 0.5 * z + 1.0
    odd = (q & 1) == 1
    cs = jnp.where(odd, s, c)
    sn = jnp.where(odd, c, s)
    return jnp.where(((q + 1) & 2) == 2, -cs, cs), jnp.where((q & 2) == 2, -sn, sn)


def circle(k, size):
    quarter = size // 4
    k = k + quarter // 2
    q = k >> (quarter.bit_length() - 1)
    r = (k & (quarter - 1)) - quarter // 2
    return turn_parts(r.astype(F32) * (2.0 * math.pi / size), q)


def poly(z, *coefficients):
    total = coefficients[-1] * z + coefficients[-2]
    for c in coefficients[-3::-1]:
        total = total * z + c
    return total


def radians(x):
    h = 0.5 * x
    z = h * h
    s = h * poly(z, 1.0, -0.1666666716337204, 0.008333330973982811, -0.00019840861205011606, 2.752528644123231e-06, -2.3889498379503493e-08)
    c = poly(z, 1.0, -0.5, 0.0416666679084301, -0.0013888884568586946, 2.4801040126476437e-05, -2.75246833325582e-07, 1.9907673287633543e-09)
    t = s + s
    return 1.0 - t * s, t * c


def split(x):
    hi = x.astype(BF16)
    return hi, (x - hi.astype(F32)).astype(BF16)


def mm(a, b, nt=False):
    dims = (((1,), (1 if nt else 0,)), ((), ()))
    return lax.dot_general(a, b, dims, preferred_element_type=F32)


def rotate(a_re, a_im, b_re, b_im):
    return a_re * b_re - a_im * b_im, a_re * b_im + a_im * b_re


def put(hi_ref, lo_ref, at, size, col, x):
    hi, lo = split(x)
    hi_ref[pl.ds(at, size), col : col + BAND] = hi
    lo_ref[pl.ds(at, size), col : col + BAND] = lo
    return hi, lo


def multiply_band(n_col, t, table, field, a_re, a_im, b_re, b_im, out):
    rows = field.shape[0] // 2
    cols = field.shape[1]
    part = BAND // (n_col * CHUNKS)
    per = part // STEP
    for j in range(0, cols, LANES):
        br = b_re[:, j : j + LANES]
        bi = b_im[:, j : j + LANES]
        for h in range(CHUNKS):
            for i in range(per):
                row = (t * CHUNKS + h) * per + i
                re, im = rotate(a_re[row : row + 1, j : j + LANES], a_im[row : row + 1, j : j + LANES], br, bi)
                at = 2 * h * part + i * STEP
                table[at : at + STEP, j : j + LANES] = re.astype(BF16)
                table[at + part : at + part + STEP, j : j + LANES] = im.astype(BF16)
    prod = mm(table[...], field[...], nt=True)
    for at in range(0, 2 * CHUNKS * part, 2 * part):
        mid = at + part
        out[at:mid, :] = prod[at:mid, :rows] - prod[mid : mid + part, rows:]
        out[mid : mid + part, :] = prod[at:mid, rows:] + prod[mid : mid + part, :rows]


def first_kernel(n_col, offs_hbm, ph_hbm, out, field, a_re, a_im, b_re, b_im, ph, offs, table, sem, ph_sem):
    rows, cols = ph.shape
    pieces = ph_sem.shape[0]
    size = rows // pieces
    get = pltpu.make_async_copy(offs_hbm, offs, sem)
    get.start()
    loads = [
        pltpu.make_async_copy(ph_hbm.at[pl.ds(i * size, size)], ph.at[pl.ds(i * size, size)], ph_sem.at[i])
        for i in range(pieces)
    ]
    for load in loads:
        load.start()
    me = lax.axis_index("col")
    n0 = me * cols
    share = BAND // n_col
    per = share // STEP
    for j in range(0, cols, LANES):
        n = n0 + j + lax.broadcasted_iota(I32, (STEP, LANES), 1)
        low = lax.broadcasted_iota(I32, (STEP, LANES), 0)
        c, s = circle((low * n) & (HOLO - 1), HOLO)
        b_re[:, j : j + LANES] = c
        b_im[:, j : j + LANES] = -s
    for i in range(pieces):
        loads[i].wait()
        for at in range(i * size, (i + 1) * size, STEP):
            for j in range(0, cols, LANES):
                c, s = radians(ph[at : at + STEP, j : j + LANES])
                field[at : at + STEP, j : j + LANES] = c.astype(BF16)
                field[rows + at : rows + at + STEP, j : j + LANES] = s.astype(BF16)
    get.wait()
    offset = offs[0, 1]
    for j in range(0, cols, LANES):
        n = n0 + j + lax.broadcasted_iota(I32, (BAND // STEP, LANES), 1)
        row = lax.broadcasted_iota(I32, (BAND // STEP, LANES), 0)
        v = (me ^ (row // per)) * share + (row % per) * STEP
        c, s = circle((((offset + v) & (HOLO - 1)) * n) & (HOLO - 1), HOLO)
        a_re[:, j : j + LANES] = c
        a_im[:, j : j + LANES] = -s
    multiply_band(n_col, n_col - 1, table, field, a_re, a_im, b_re, b_im, out)


def later_kernel(n_col, t, field, a_re, a_im, b_re, b_im, out, table):
    multiply_band(n_col, t, table, field, a_re, a_im, b_re, b_im, out)


def lens_table_kernel(
    n_row, n_col, n_pupil, spacing, offs_hbm, codes_hbm, fl_hi, fl_lo, lens_hi, lens_lo, ev, a_re, a_im, offs, codes, sems
):
    gets = [
        pltpu.make_async_copy(offs_hbm, offs, sems.at[0]),
        pltpu.make_async_copy(codes_hbm, codes, sems.at[1]),
    ]
    for get in gets:
        get.start()
    depths = codes.shape[0]
    r, c, p = (lax.axis_index(a) for a in ("row", "col", "pupil"))
    own = depths // n_pupil
    xs = BAND // (n_row * n_col)
    share = BAND // n_col
    part = share // CHUNKS
    big = 4 * (BAND // 2) ** 2
    scale = 1.0 / math.sqrt(BAND)
    for get in gets:
        get.wait()
    offset = offs[0, 0]
    rows_here = fl_hi.shape[0] // n_row
    per = rows_here // STEP
    blocks = a_re.shape[0]
    row = lax.broadcasted_iota(I32, (blocks, BAND), 0)
    freq = (offset + lax.broadcasted_iota(I32, (blocks, BAND), 1)) & (HOLO - 1)
    m = (r ^ (row // per)) * rows_here + (row % per) * STEP
    cs, sn = circle((freq * (m * spacing)) & (HOLO - 1), HOLO)
    a_re[...] = cs
    a_im[...] = -sn
    low = lax.broadcasted_iota(I32, (STEP, BAND), 0)
    freq = (offset + lax.broadcasted_iota(I32, (STEP, BAND), 1)) & (HOLO - 1)
    b_re, b_im = circle((freq * (low * spacing)) & (HOLO - 1), HOLO)
    b_im = -b_im

    def fill(i, _):
        at = pl.multiple_of(i * STEP, STEP)
        re, im = rotate(a_re[pl.ds(i, 1), :], a_im[pl.ds(i, 1), :], b_re, b_im)
        put(fl_hi, fl_lo, at, STEP, 0, re)
        put(fl_hi, fl_lo, at, STEP, BAND, im)
        return 0

    lax.fori_loop(0, blocks, fill, 0, unroll=4)
    code = [codes[((d // own) ^ p) * own + d % own] for d in range(depths)]
    u = lax.broadcasted_iota(I32, (1, BAND), 1) - BAND // 2
    turn = [circle((code[d] * (u * u)) & (big - 1), big) for d in range(depths)]
    for t in range(n_col):
        x = (r * n_col + (c ^ t)) * xs + lax.broadcasted_iota(I32, (xs, BAND), 0)
        uu = lax.broadcasted_iota(I32, (xs, BAND), 1)
        g_re, g_im = circle((x * uu) & (BAND - 1), BAND)
        g_re = g_re * scale
        g_im = g_im * scale
        for d in range(depths):
            re, im = rotate(g_re, g_im, *turn[d])
            at = (t * depths + d) * xs
            put(lens_hi, lens_lo, at, xs, 0, re)
            put(lens_hi, lens_lo, at, xs, BAND, im)
    lane = lax.broadcasted_iota(I32, (1, 2 * part), 1)
    for h in range(CHUNKS):
        v = c * share + h * part + lane % part - BAND // 2
        for d in range(depths):
            e_re, e_im = circle((code[d] * (v * v)) & (big - 1), big)
            at = 2 * (h * depths + d)
            ev[at : at + 1, :] = e_re
            ev[at + 1 : at + 2, :] = jnp.where(lane < part, -e_im, e_im)


def image_table_kernel(n_col, *refs):
    c = lax.axis_index("col")
    share = BAND // n_col
    part = share // CHUNKS
    per = part // STEP
    scale = 1.0 / math.sqrt(BAND)
    a_re, a_im = refs[2 * CHUNKS :]
    row = lax.broadcasted_iota(I32, a_re.shape, 0)
    y = lax.broadcasted_iota(I32, a_re.shape, 1)
    v = (c ^ ((row // per) % n_col)) * share + (row // (per * n_col)) * part + (row % per) * STEP
    cs, sn = circle((v * y) & (BAND - 1), BAND)
    a_re[...] = cs
    a_im[...] = sn
    low = lax.broadcasted_iota(I32, (STEP, BAND), 0)
    y = lax.broadcasted_iota(I32, (STEP, BAND), 1)
    b_re, b_im = circle((low * y) & (BAND - 1), BAND)
    b_re = b_re * scale
    b_im = b_im * scale
    for h in range(CHUNKS):
        g_hi, g_lo = refs[2 * h : 2 * h + 2]
        for t in range(n_col):
            for i in range(per):
                row = (h * n_col + t) * per + i
                re, im = rotate(a_re[row : row + 1, :], a_im[row : row + 1, :], b_re, b_im)
                at = 2 * t * part + i * STEP
                hi, lo = put(g_hi, g_lo, at, STEP, 0, re)
                g_hi[at + part : at + part + STEP, BAND:] = hi
                g_lo[at + part : at + part + STEP, BAND:] = lo
                hi, lo = put(g_hi, g_lo, at, STEP, BAND, im)
                g_hi[at + part : at + part + STEP, :BAND] = -hi
                g_lo[at + part : at + part + STEP, :BAND] = -lo


def lens_kernel(n_row, n_col, depths, chunk, *refs):
    halves = refs[:n_row]
    fl_hi, fl_lo, lens_hi, lens_lo, ev = refs[n_row : n_row + 5]
    outs = refs[n_row + 5 : n_row + 5 + n_col]
    x2, w2 = refs[n_row + 5 + n_col :]
    part = BAND // (n_col * CHUNKS)
    both = 2 * part
    xs = BAND // (n_row * n_col)
    rows_here = halves[0].shape[1]
    for i, h in enumerate(halves):
        hi, lo = split(h[...])
        x2[:both, i * rows_here : (i + 1) * rows_here] = hi
        x2[both:, i * rows_here : (i + 1) * rows_here] = lo
    s = mm(x2[...], fl_hi[...])
    s = s[:both] + (s[both:] + mm(x2[:both, :], fl_lo[...]))
    s_re = (s[:part, :BAND] - s[part:, BAND:]) * (1.0 / HOLO)
    s_im = (s[:part, BAND:] + s[part:, :BAND]) * (1.0 / HOLO)
    hi, lo = split(s_re)
    w2[:part, :BAND] = hi
    w2[part:both, BAND:] = hi
    w2[both : both + part, :BAND] = lo
    w2[both + part :, BAND:] = lo
    hi, lo = split(s_im)
    w2[part:both, :BAND] = hi
    w2[:part, BAND:] = -hi
    w2[both + part :, :BAND] = lo
    w2[both : both + part, BAND:] = -lo
    block = depths * xs
    for t in list(range(1, n_col)) + [0]:
        at = t * block
        z = mm(lens_hi[at : at + block, :], w2[...], nt=True)
        z = z[:, :both] + (z[:, both:] + mm(lens_lo[at : at + block, :], w2[:both, :], nt=True))
        for d in range(depths):
            piece = z[d * xs : (d + 1) * xs, :]
            row = 2 * (chunk * depths + d)
            turned = piece * ev[row : row + 1, :] + pltpu.roll(piece, part, 1) * ev[row + 1 : row + 2, :]
            outs[t][d * xs : (d + 1) * xs, :] = turned


def image_sum(blocks, g_hi, g_lo, lo_rows, hi_rows):
    x = jnp.concatenate([b[lo_rows:hi_rows, :] for b in blocks], axis=1)
    hi, lo = split(x)
    return mm(hi, g_hi[...]) + (mm(lo, g_hi[...]) + mm(hi, g_lo[...]))


def image_kernel(n_col, *refs):
    refs[-1][...] = image_sum(refs[:n_col], refs[n_col], refs[n_col + 1], 0, refs[0].shape[0])


def power_kernel(n_col, lo_rows, hi_rows, *refs):
    z = image_sum(refs[:n_col], refs[n_col], refs[n_col + 1], lo_rows, hi_rows)
    for more in refs[n_col + 2 : -1]:
        z = z + more[lo_rows:hi_rows, :]
    re = z[:, :BAND]
    im = z[:, BAND:]
    refs[-1][...] = re * re + im * im


def spec(shape, dtype=F32):
    return jax.ShapeDtypeStruct(shape, dtype)


def call(kernel, outs, ins, scratch=(), hbm=0, mib=16):
    vm = pl.BlockSpec(memory_space=pltpu.VMEM)
    return pl.pallas_call(
        kernel,
        out_shape=outs,
        in_specs=[pl.BlockSpec(memory_space=pltpu.HBM)] * hbm + [vm] * (ins - hbm),
        out_specs=[vm] * len(outs),
        scratch_shapes=list(scratch),
        compiler_params=pltpu.CompilerParams(vmem_limit_bytes=mib * 1024 * 1024),
    )


def in_hbm(x):
    return pltpu.with_memory_space_constraint(x, pltpu.HBM)


def swap(x, axis, t):
    n = lax.axis_size(axis)
    return lax.ppermute(x, axis, [(i, i ^ t) for i in range(n)])


def local(phase, band_offsets, depth_codes):
    rows, cols = phase.shape
    n_row, n_col, n_pupil = (lax.axis_size(a) for a in ("row", "col", "pupil"))
    depths = depth_codes.shape[0]
    own = depths // n_pupil
    share = BAND // n_col
    part = share // CHUNKS
    xs = BAND // (n_row * n_col)
    block = depths * xs
    spacing = HOLO // (rows * n_row)
    dma = pltpu.SemaphoreType.DMA
    away = range(n_col - 1, 0, -1)

    piece = spec((2 * share, rows))
    table = pltpu.VMEM((2 * share, cols), BF16)
    offs = in_hbm(band_offsets)
    first = call(
        functools.partial(first_kernel, n_col),
        [piece, spec((2 * rows, cols), BF16)] + [spec((BAND // STEP, cols))] * 2 + [spec((STEP, cols))] * 2,
        2,
        [pltpu.VMEM((rows, cols), F32), pltpu.SMEM(band_offsets.shape, I32), table, dma, dma((4,))],
        2,
    )(offs, in_hbm(phase))
    got = [swap(first[0], "col", n_col - 1)]
    for t in range(n_col - 2, -1, -1):
        x = call(functools.partial(later_kernel, n_col, t), [piece], 5, [table])(*first[1:])[0]
        got.append(swap(x, "col", t) if t else x)

    blocks = n_row * rows // STEP
    lens_tables = call(
        functools.partial(lens_table_kernel, n_row, n_col, n_pupil, spacing),
        [spec((n_row * rows, 2 * BAND), BF16)] * 2
        + [spec((n_col * block, 2 * BAND), BF16)] * 2
        + [spec((2 * CHUNKS * depths, 2 * part))],
        2,
        [pltpu.VMEM((blocks, BAND), F32)] * 2
        + [pltpu.SMEM(band_offsets.shape, I32), pltpu.SMEM(depth_codes.shape, I32), dma((2,))],
        2,
    )
    tables = lens_tables(offs, in_hbm(depth_codes))
    image_tables = call(
        functools.partial(image_table_kernel, n_col),
        [spec((2 * n_col * part, 2 * BAND), BF16)] * (2 * CHUNKS),
        0,
        [pltpu.VMEM((BAND // STEP, BAND), F32)] * 2,
    )()

    sums = []
    blocks = []
    for h in range(CHUNKS):
        half = got[-1][2 * h * part : 2 * (h + 1) * part]
        for x in got[:-1]:
            half = half + x[2 * h * part : 2 * (h + 1) * part]
        halves = [half] + [swap(half, "row", t) for t in range(1, n_row)]
        lens = call(
            functools.partial(lens_kernel, n_row, n_col, depths, h),
            [spec((block, 2 * part))] * n_col,
            n_row + 5,
            [pltpu.VMEM((4 * part, n_row * rows), BF16), pltpu.VMEM((4 * part, 2 * BAND), BF16)],
        )(*halves, *tables)
        blocks.append([lens[0]] + [swap(lens[t], "col", t) for t in away][::-1])
    for h in range(CHUNKS - 1):
        sums.append(
            call(functools.partial(image_kernel, n_col), [spec((block, 2 * BAND))], n_col + 2)(
                *blocks[h], *image_tables[2 * h : 2 * h + 2]
            )[0]
        )
    size = block // n_pupil
    power = {}
    for t in list(range(1, n_pupil)) + [0]:
        power[t] = call(
            functools.partial(power_kernel, n_col, t * size, (t + 1) * size),
            [spec((size, BAND))],
            n_col + 2 + len(sums),
        )(*blocks[-1], *image_tables[-2:], *sums)[0]
    total = power[0]
    for t in range(1, n_pupil):
        total = total + swap(power[t], "pupil", t)
    total = total * (1.0 / (band_offsets.shape[0] * n_pupil))
    return total.reshape(own, xs, BAND)


def solution(mesh):
    in_specs = (P("row", "col"), P("pupil", None), P())
    out_specs = P("pupil", ("row", "col"), None)
    return jax.shard_map(local, mesh=mesh, in_specs=in_specs, out_specs=out_specs, check_vma=False)
```

time: 53.3 us -> 48 us (0.901)
  the two profiles are of different devices: /device:TPU:17 before, /device:TPU:0 now
where the time goes in v1:
time: 48 us; the launch traced here: 47.8 us
  starting transfers between devices  21.5 us (45%)
  Pallas kernels  14.4 us (30%)
  waiting for transfers between devices  11 us (23%)
  other arithmetic  0.77 us (2%)
    ppermute x16, starting transfers between devices, swap(): return lax.ppermute(x, axis, [(i, i ^ t) for i in range(n)])  21.5 us
    ppermute x16, waiting for transfers between devices, swap(): return lax.ppermute(x, axis, [(i, i ^ t) for i in range(n)])  11 us
    pallas_call x2, Pallas kernels, local(): call(functools.partial(lens_kernel, n_row, n_col, depths, h), [spec((bloc...  3.8 us
    pallas_call x1, Pallas kernels, local(): tables = lens_tables(offs, in_hbm(depth_codes))  3.31 us
    pallas_call x1, Pallas kernels, local(): call(functools.partial(first_kernel, n_col), [piece, spec((2 * rows, cols...  2.89 us
    pallas_call x3, Pallas kernels, local(): call(functools.partial(later_kernel, n_col, t), [piece], 5, [table])  1.53 us
    pallas_call x2, Pallas kernels, local(): call(functools.partial(power_kernel, n_col, t * size, (t + 1) * size), [s...  1.17 us
    pallas_call x1, Pallas kernels, local(): call(functools.partial(image_kernel, n_col), [spec((block, 2 * BAND))], n...  0.97 us
  transfers between devices with their start and end apart: 16, of which 9 were waited for; matrix products, arithmetic and copies ran while one was open for 0% of the time, Pallas kernels for 18%

profile of v1, /device:TPU:0, one launch (start us, length us, event | category | flops | bytes accessed | tf_op | source)
XLA Modules:
  0.0 47.8 jit_solution(14442402374127058479)
XLA Ops:
  0.0 2.9 %shard_map.37 = (f32[256,128]{1,0:T(8,128)S(1)}, bf16[256,2048]{1,0:T(8,128)(2,1)S(1)}, f32[32,2048]{1,0:T(8,128)S(1)}, f32[32,2048]{1,0:T(8,128)S(1)}, f32[16,2048]{1,0:T(8,128)S(1)}, /*index=5*/f32[16,2048]{1,0:T(8,128)S(1)}) custom-call(s32[1,2]{1,0:T(1,128)} %offs_hbm.3, f32[128,2048]{1,0:T(8,128)} %ph_hbm.1), custom_call_target="tpu_custom_call" | custom-call | tf_op jit(solution)/shard_map/pallas_call | solution.py:342
  2.9 0.5 %shard_map.39 = f32[256,128]{1,0:T(8,128)S(1)} custom-call(bf16[256,2048]{1,0:T(8,128)(2,1)S(1)} %get-tuple-element.28.field, f32[32,2048]{1,0:T(8,128)S(1)} %get-tuple-element.29.a_re, f32[32,2048]{1,0:T(8,128)S(1)} %get-tuple-element.30.a_im, f32[16,2048]{1,0:T(8,128)S(1)} %get-tuple-element.31.b_re, f32[16,2048]{1,0:T(8,128)S(1)} %get-tuple-element.32.b_im), custom_call_target="tpu_custom_call" | custom-call | tf_op jit(solution)/shard_map/pallas_call | solution.py:351
  3.4 3.1 %collective-permute-start.1 = (f32[256,128]{1,0:T(8,128)S(1)}, f32[256,128]{1,0:T(8,128)S(1)}, u32[]{:S(2)}, u32[]{:S(2)}) collective-permute-start(f32[256,128]{1,0:T(8,128)S(1)} %shard_map.39), channel_id=1, source_target_pairs={{0,4},{2,6},{4,0},{6,2},{1,5},{3,7},{5,1},{7,3},{8,12},{10,14},{12... | collective-permute-start | bytes 393224 | tf_op jit(solution)/shard_map/ppermute | solution.py:323
  6.5 0.5 %shard_map.40 = f32[256,128]{1,0:T(8,128)S(1)} custom-call(bf16[256,2048]{1,0:T(8,128)(2,1)S(1)} %get-tuple-element.28.field, f32[32,2048]{1,0:T(8,128)S(1)} %get-tuple-element.29.a_re, f32[32,2048]{1,0:T(8,128)S(1)} %get-tuple-element.30.a_im, f32[16,2048]{1,0:T(8,128)S(1)} %get-tuple-element.31.b_re, f32[16,2048]{1,0:T(8,128)S(1)} %get-tuple-element.32.b_im), custom_call_target="tpu_custom_call" | custom-call | tf_op jit(solution)/shard_map/pallas_call | solution.py:351
  7.0 1.6 %collective-permute-start.2 = (f32[256,128]{1,0:T(8,128)S(1)}, f32[256,128]{1,0:T(8,128)S(1)}, u32[]{:S(2)}, u32[]{:S(2)}) collective-permute-start(f32[256,128]{1,0:T(8,128)S(1)} %shard_map.40), channel_id=1, source_target_pairs={{0,2},{2,0},{4,6},{6,4},{1,3},{3,1},{5,7},{7,5},{8,10},{10,8},{12,... | collective-permute-start | bytes 393224 | tf_op jit(solution)/shard_map/ppermute | solution.py:323
  8.6 0.0 collective-permute-start
  8.6 0.5 %shard_map.38 = f32[256,128]{1,0:T(8,128)S(1)} custom-call(bf16[256,2048]{1,0:T(8,128)(2,1)S(1)} %get-tuple-element.28.field, f32[32,2048]{1,0:T(8,128)S(1)} %get-tuple-element.29.a_re, f32[32,2048]{1,0:T(8,128)S(1)} %get-tuple-element.30.a_im, f32[16,2048]{1,0:T(8,128)S(1)} %get-tuple-element.31.b_re, f32[16,2048]{1,0:T(8,128)S(1)} %get-tuple-element.32.b_im), custom_call_target="tpu_custom_call" | custom-call | tf_op jit(solution)/shard_map/pallas_call | solution.py:351
  9.1 0.9 %collective-permute-done.1 = f32[256,128]{1,0:T(8,128)S(1)} collective-permute-done((f32[256,128]{1,0:T(8,128)S(1)}, f32[256,128]{1,0:T(8,128)S(1)}, u32[]{:S(2)}, u32[]{:S(2)}) %collective-permute-start.1) | collective-permute-done | bytes 131104 | tf_op jit(solution)/shard_map/ppermute | solution.py:323
  10.0 3.4 %collective-permute-done.2 = f32[256,128]{1,0:T(8,128)S(1)} collective-permute-done((f32[256,128]{1,0:T(8,128)S(1)}, f32[256,128]{1,0:T(8,128)S(1)}, u32[]{:S(2)}, u32[]{:S(2)}) %collective-permute-start.2) | collective-permute-done | bytes 131104 | tf_op jit(solution)/shard_map/ppermute | solution.py:323
  13.4 1.1 %collective-permute-done = f32[256,128]{1,0:T(8,128)S(1)} collective-permute-done((f32[256,128]{1,0:T(8,128)S(1)}, f32[256,128]{1,0:T(8,128)S(1)}, u32[]{:S(2)}, u32[]{:S(2)}) %collective-permute-start) | collective-permute-done | bytes 131104 | tf_op jit(solution)/shard_map/ppermute | solution.py:323
  14.6 3.9 %collective-permute-start.11 = (f32[128,128]{1,0:T(8,128)S(1)}, f32[128,128]{1,0:T(8,128)S(1)}, u32[]{:S(2)}, u32[]{:S(2)}) collective-permute-start(f32[128,128]{1,0:T(8,128)S(1)} %get-tuple-element.51.refs_0_), channel_id=1, source_target_pairs={{0,24},{8,16},{16,8},{24,0},{1,25},{9,17},{17,9},{25,1},{2,26},{10... | collective-permute-start | bytes 196616 | tf_op jit(solution)/shard_map/ppermute | solution.py:323
  18.5 0.0 collective-permute-start.10
  18.5 0.6 %collective-permute-start.9 = (f32[128,128]{1,0:T(8,128)S(1)}, f32[128,128]{1,0:T(8,128)S(1)}, u32[]{:S(2)}, u32[]{:S(2)}) collective-permute-start(f32[128,128]{1,0:T(8,128)S(1)} %get-tuple-element.51.refs_0_), channel_id=1, source_target_pairs={{0,8},{8,0},{16,24},{24,16},{1,9},{9,1},{17,25},{25,17},{2,10},{10... | collective-permute-start | bytes 196616 | tf_op jit(solution)/shard_map/ppermute | solution.py:323
  19.1 3.3 %shard_map.41 = (bf16[512,1024]{1,0:T(8,128)(2,1)S(1)}, bf16[512,1024]{1,0:T(8,128)(2,1)S(1)}, bf16[1024,1024]{1,0:T(8,128)(2,1)S(1)}, bf16[1024,1024]{1,0:T(8,128)(2,1)S(1)}, f32[32,128]{1,0:T(8,128)S(1)}) custom-call(s32[1,2]{1,0:T(1,128)} %offs_hbm.3, s32[8]{0:T(128)} %codes_hbm.1), custom_call_target="tpu_custom_call" | custom-call | tf_op jit(solution)/shard_map/pallas_call | solution.py:365
  22.4 0.0 collective-permute-done.11.refs_3_
  22.4 1.4 %collective-permute-done.10.refs_2_ = f32[128,128]{1,0:T(8,128)S(1)} collective-permute-done((f32[128,128]{1,0:T(8,128)S(1)}, f32[128,128]{1,0:T(8,128)S(1)}, u32[]{:S(2)}, u32[]{:S(2)}) %collective-permute-start.10) | collective-permute-done | bytes 65568 | tf_op jit(solution)/shard_map/ppermute | solution.py:323
  23.8 0.0 collective-permute-done.9.refs_1_
  23.8 1.9 %shard_map.44 = (f32[256,128]{1,0:T(8,128)S(1)}, f32[256,128]{1,0:T(8,128)S(1)}, f32[256,128]{1,0:T(8,128)S(1)}, f32[256,128]{1,0:T(8,128)S(1)}) custom-call(f32[128,128]{1,0:T(8,128)S(1)} %get-tuple-element.51.refs_0_, f32[128,128]{1,0:T(8,128)S(1)} %collective-permute-done.9.refs_1_, f32[128,128]{1,0:T(8,128)S(1)} %collective-permute-done.10.refs_2_, ...), custom_call_target="tpu_custom_call" | custom-call | tf_op jit(solution)/shard_map/pallas_call | solution.py:380
  25.7 1.4 %collective-permute-start.12 = (f32[256,128]{1,0:T(8,128)S(1)}, f32[256,128]{1,0:T(8,128)S(1)}, u32[]{:S(2)}, u32[]{:S(2)}) collective-permute-start(f32[256,128]{1,0:T(8,128)S(1)} %get-tuple-element.46), channel_id=1, source_target_pairs={{0,2},{2,0},{4,6},{6,4},{1,3},{3,1},{5,7},{7,5},{8,10},{10,8},{12,... | collective-permute-start | bytes 393224 | tf_op jit(solution)/shard_map/ppermute | solution.py:323
  27.1 2.6 %collective-permute-start.5 = (f32[128,128]{1,0:T(8,128)S(1)}, f32[128,128]{1,0:T(8,128)S(1)}, u32[]{:S(2)}, u32[]{:S(2)}) collective-permute-start(f32[128,128]{1,0:T(8,128)S(1)} %get-tuple-element.52.refs_0_), channel_id=1, source_target_pairs={{0,24},{8,16},{16,8},{24,0},{1,25},{9,17},{17,9},{25,1},{2,26},{10... | collective-permute-start | bytes 196616 | tf_op jit(solution)/shard_map/ppermute | solution.py:323
  29.7 0.0 collective-permute-start.4
  29.7 1.8 %collective-permute-start.3 = (f32[128,128]{1,0:T(8,128)S(1)}, f32[128,128]{1,0:T(8,128)S(1)}, u32[]{:S(2)}, u32[]{:S(2)}) collective-permute-start(f32[128,128]{1,0:T(8,128)S(1)} %get-tuple-element.52.refs_0_), channel_id=1, source_target_pairs={{0,8},{8,0},{16,24},{24,16},{1,9},{9,1},{17,25},{25,17},{2,10},{10... | collective-permute-start | bytes 196616 | tf_op jit(solution)/shard_map/ppermute | solution.py:323
  31.5 1.5 %collective-permute-start.13 = (f32[256,128]{1,0:T(8,128)S(1)}, f32[256,128]{1,0:T(8,128)S(1)}, u32[]{:S(2)}, u32[]{:S(2)}) collective-permute-start(f32[256,128]{1,0:T(8,128)S(1)} %get-tuple-element.47), channel_id=1, source_target_pairs={{0,4},{2,6},{4,0},{6,2},{1,5},{3,7},{5,1},{7,3},{8,12},{10,14},{12... | collective-permute-start | bytes 393224 | tf_op jit(solution)/shard_map/ppermute | solution.py:323
  33.0 0.2 collective-permute-done.5.refs_3_
  33.2 1.5 %collective-permute-start.14 = (f32[256,128]{1,0:T(8,128)S(1)}, f32[256,128]{1,0:T(8,128)S(1)}, u32[]{:S(2)}, u32[]{:S(2)}) collective-permute-start(f32[256,128]{1,0:T(8,128)S(1)} %get-tuple-element.48), channel_id=1, source_target_pairs={{0,6},{2,4},{4,2},{6,0},{1,7},{3,5},{5,3},{7,1},{8,14},{10,12},{12... | collective-permute-start | bytes 393224 | tf_op jit(solution)/shard_map/ppermute | solution.py:323
  34.6 0.3 collective-permute-done.4.refs_2_
  35.0 0.0 collective-permute-done.3.refs_1_
  35.0 1.9 %shard_map.42 = (f32[256,128]{1,0:T(8,128)S(1)}, f32[256,128]{1,0:T(8,128)S(1)}, f32[256,128]{1,0:T(8,128)S(1)}, f32[256,128]{1,0:T(8,128)S(1)}) custom-call(f32[128,128]{1,0:T(8,128)S(1)} %get-tuple-element.52.refs_0_, f32[128,128]{1,0:T(8,128)S(1)} %collective-permute-done.3.refs_1_, f32[128,128]{1,0:T(8,128)S(1)} %collective-permute-done.4.refs_2_, ...), custom_call_target="tpu_custom_call" | custom-call | tf_op jit(solution)/shard_map/pallas_call | solution.py:380
  36.9 1.2 %collective-permute-start.6 = (f32[256,128]{1,0:T(8,128)S(1)}, f32[256,128]{1,0:T(8,128)S(1)}, u32[]{:S(2)}, u32[]{:S(2)}) collective-permute-start(f32[256,128]{1,0:T(8,128)S(1)} %get-tuple-element.40), channel_id=1, source_target_pairs={{0,2},{2,0},{4,6},{6,4},{1,3},{3,1},{5,7},{7,5},{8,10},{10,8},{12,... | collective-permute-start | bytes 393224 | tf_op jit(solution)/shard_map/ppermute | solution.py:323
  38.1 0.9 %collective-permute-start.7 = (f32[256,128]{1,0:T(8,128)S(1)}, f32[256,128]{1,0:T(8,128)S(1)}, u32[]{:S(2)}, u32[]{:S(2)}) collective-permute-start(f32[256,128]{1,0:T(8,128)S(1)} %get-tuple-element.41), channel_id=1, source_target_pairs={{0,4},{2,6},{4,0},{6,2},{1,5},{3,7},{5,1},{7,3},{8,12},{10,14},{12... | collective-permute-start | bytes 393224 | tf_op jit(solution)/shard_map/ppermute | solution.py:323
  39.0 0.0 collective-permute-done.12.refs_1_
  39.0 1.4 %collective-permute-start.8 = (f32[256,128]{1,0:T(8,128)S(1)}, f32[256,128]{1,0:T(8,128)S(1)}, u32[]{:S(2)}, u32[]{:S(2)}) collective-permute-start(f32[256,128]{1,0:T(8,128)S(1)} %get-tuple-element.42), channel_id=1, source_target_pairs={{0,6},{2,4},{4,2},{6,0},{1,7},{3,5},{5,3},{7,1},{8,14},{10,12},{12... | collective-permute-start | bytes 393224 | tf_op jit(solution)/shard_map/ppermute | solution.py:323
  40.5 0.7 %shard_map.43 = (bf16[512,1024]{1,0:T(8,128)(2,1)S(1)}, bf16[512,1024]{1,0:T(8,128)(2,1)S(1)}, bf16[512,1024]{1,0:T(8,128)(2,1)S(1)}, bf16[512,1024]{1,0:T(8,128)(2,1)S(1)}) custom-call(), custom_call_target="tpu_custom_call" | custom-call | tf_op jit(solution)/shard_map/pallas_call | solution.py:366
  41.2 0.0 collective-permute-done.13.refs_2_
  41.2 0.0 collective-permute-done.14.refs_3_
  41.2 1.0 %shard_map.45.refs_6_ = f32[256,1024]{1,0:T(8,128)S(1)} custom-call(f32[256,128]{1,0:T(8,128)S(1)} %get-tuple-element.45.refs_0_, f32[256,128]{1,0:T(8,128)S(1)} %collective-permute-done.12.refs_1_, f32[256,128]{1,0:T(8,128)S(1)} %collective-permute-done.13.refs_2_, f32[256,128]{1,0:T(8,128)S(1)} %collective-permute-done.14.refs_3_, ...), custom_call_target="tpu_custom_call" | custom-call | tf_op jit(solution)/shard_map/pallas_call | solution.py:389
  42.2 0.0 collective-permute-done.6.refs_1_
  42.2 1.1 %collective-permute-done.7.refs_2_ = f32[256,128]{1,0:T(8,128)S(1)} collective-permute-done((f32[256,128]{1,0:T(8,128)S(1)}, f32[256,128]{1,0:T(8,128)S(1)}, u32[]{:S(2)}, u32[]{:S(2)}) %collective-permute-start.7) | collective-permute-done | bytes 131104 | tf_op jit(solution)/shard_map/ppermute | solution.py:323
  43.3 1.5 %collective-permute-done.8.refs_3_ = f32[256,128]{1,0:T(8,128)S(1)} collective-permute-done((f32[256,128]{1,0:T(8,128)S(1)}, f32[256,128]{1,0:T(8,128)S(1)}, u32[]{:S(2)}, u32[]{:S(2)}) %collective-permute-start.8) | collective-permute-done | bytes 131104 | tf_op jit(solution)/shard_map/ppermute | solution.py:323
  44.9 0.6 %shard_map.47 = f32[128,512]{1,0:T(8,128)S(1)} custom-call(f32[256,128]{1,0:T(8,128)S(1)} %get-tuple-element.39.refs_0_, f32[256,128]{1,0:T(8,128)S(1)} %collective-permute-done.6.refs_1_, f32[256,128]{1,0:T(8,128)S(1)} %collective-permute-done.7.refs_2_, f32[256,128]{1,0:T(8,128)S(1)} %collective-permute-done.8.refs_3_, ...), custom_call_target="tpu_custom_call" | custom-call | tf_op jit(solution)/shard_map/pallas_call | solution.py:396
  45.5 0.1 collective-permute-start.15
  45.6 0.6 %shard_map.46 = f32[128,512]{1,0:T(8,128)S(1)} custom-call(f32[256,128]{1,0:T(8,128)S(1)} %get-tuple-element.39.refs_0_, f32[256,128]{1,0:T(8,128)S(1)} %collective-permute-done.6.refs_1_, f32[256,128]{1,0:T(8,128)S(1)} %collective-permute-done.7.refs_2_, f32[256,128]{1,0:T(8,128)S(1)} %collective-permute-done.8.refs_3_, ...), custom_call_target="tpu_custom_call" | custom-call | tf_op jit(solution)/shard_map/pallas_call | solution.py:396
  46.1 0.9 %collective-permute-done.15 = f32[128,512]{1,0:T(8,128)S(1)} collective-permute-done((f32[128,512]{1,0:T(8,128)S(1)}, f32[128,512]{1,0:T(8,128)S(1)}, u32[]{:S(2)}, u32[]{:S(2)}) %collective-permute-start.15) | collective-permute-done | bytes 262176 | tf_op jit(solution)/shard_map/ppermute | solution.py:323
  47.1 0.7 %add_multiply_fusion = f32[128,512]{1,0:T(8,128)} fusion(f32[128,512]{1,0:T(8,128)S(1)} %shard_map.46, f32[128,512]{1,0:T(8,128)S(1)} %collective-permute-done.15), kind=kLoop, calls=%fused_computation | loop fusion | flops 131072 | bytes 786432 | tf_op jit(solution)/shard_map/mul | solution.py:404
  (1 shorter events, 0.0 us)
Async XLA Ops:
  3.4 6.6 %collective-permute-start.1 = (f32[256,128]{1,0:T(8,128)S(1)}, f32[256,128]{1,0:T(8,128)S(1)}, u32[]{:S(2)}, u32[]{:S(2)}) collective-permute-start(f32[256,128]{1,0:T(8,128)S(1)} %shard_map.39), channel_id=1, source_target_pairs={{0,4},{2,6},{4,0},{6,2},{1,5},{3,7},{5,1},{7,3},{8,12},{10,14},{12... | collective-permute-start | bytes 393224 | tf_op jit(solution)/shard_map/ppermute | solution.py:323
  7.0 6.4 %collective-permute-start.2 = (f32[256,128]{1,0:T(8,128)S(1)}, f32[256,128]{1,0:T(8,128)S(1)}, u32[]{:S(2)}, u32[]{:S(2)}) collective-permute-start(f32[256,128]{1,0:T(8,128)S(1)} %shard_map.40), channel_id=1, source_target_pairs={{0,2},{2,0},{4,6},{6,4},{1,3},{3,1},{5,7},{7,5},{8,10},{10,8},{12,... | collective-permute-start | bytes 393224 | tf_op jit(solution)/shard_map/ppermute | solution.py:323
  8.6 6.0 %collective-permute-start = (f32[256,128]{1,0:T(8,128)S(1)}, f32[256,128]{1,0:T(8,128)S(1)}, u32[]{:S(2)}, u32[]{:S(2)}) collective-permute-start(f32[256,128]{1,0:T(8,128)S(1)} %get-tuple-element.33), channel_id=1, source_target_pairs={{0,6},{2,4},{4,2},{6,0},{1,7},{3,5},{5,3},{7,1},{8,14},{10,12},{12... | collective-permute-start | bytes 393224 | tf_op jit(solution)/shard_map/ppermute | solution.py:323
  14.6 7.8 %collective-permute-start.11 = (f32[128,128]{1,0:T(8,128)S(1)}, f32[128,128]{1,0:T(8,128)S(1)}, u32[]{:S(2)}, u32[]{:S(2)}) collective-permute-start(f32[128,128]{1,0:T(8,128)S(1)} %get-tuple-element.51.refs_0_), channel_id=1, source_target_pairs={{0,24},{8,16},{16,8},{24,0},{1,25},{9,17},{17,9},{25,1},{2,26},{10... | collective-permute-start | bytes 196616 | tf_op jit(solution)/shard_map/ppermute | solution.py:323
  18.5 5.4 %collective-permute-start.10 = (f32[128,128]{1,0:T(8,128)S(1)}, f32[128,128]{1,0:T(8,128)S(1)}, u32[]{:S(2)}, u32[]{:S(2)}) collective-permute-start(f32[128,128]{1,0:T(8,128)S(1)} %get-tuple-element.51.refs_0_), channel_id=1, source_target_pairs={{0,16},{8,24},{16,0},{24,8},{1,17},{9,25},{17,1},{25,9},{2,18},{10... | collective-permute-start | bytes 196616 | tf_op jit(solution)/shard_map/ppermute | solution.py:323
  18.5 5.4 %collective-permute-start.9 = (f32[128,128]{1,0:T(8,128)S(1)}, f32[128,128]{1,0:T(8,128)S(1)}, u32[]{:S(2)}, u32[]{:S(2)}) collective-permute-start(f32[128,128]{1,0:T(8,128)S(1)} %get-tuple-element.51.refs_0_), channel_id=1, source_target_pairs={{0,8},{8,0},{16,24},{24,16},{1,9},{9,1},{17,25},{25,17},{2,10},{10... | collective-permute-start | bytes 196616 | tf_op jit(solution)/shard_map/ppermute | solution.py:323
  25.7 13.3 %collective-permute-start.12 = (f32[256,128]{1,0:T(8,128)S(1)}, f32[256,128]{1,0:T(8,128)S(1)}, u32[]{:S(2)}, u32[]{:S(2)}) collective-permute-start(f32[256,128]{1,0:T(8,128)S(1)} %get-tuple-element.46), channel_id=1, source_target_pairs={{0,2},{2,0},{4,6},{6,4},{1,3},{3,1},{5,7},{7,5},{8,10},{10,8},{12,... | collective-permute-start | bytes 393224 | tf_op jit(solution)/shard_map/ppermute | solution.py:323
  27.1 6.1 %collective-permute-start.5 = (f32[128,128]{1,0:T(8,128)S(1)}, f32[128,128]{1,0:T(8,128)S(1)}, u32[]{:S(2)}, u32[]{:S(2)}) collective-permute-start(f32[128,128]{1,0:T(8,128)S(1)} %get-tuple-element.52.refs_0_), channel_id=1, source_target_pairs={{0,24},{8,16},{16,8},{24,0},{1,25},{9,17},{17,9},{25,1},{2,26},{10... | collective-permute-start | bytes 196616 | tf_op jit(solution)/shard_map/ppermute | solution.py:323
  29.7 5.3 %collective-permute-start.4 = (f32[128,128]{1,0:T(8,128)S(1)}, f32[128,128]{1,0:T(8,128)S(1)}, u32[]{:S(2)}, u32[]{:S(2)}) collective-permute-start(f32[128,128]{1,0:T(8,128)S(1)} %get-tuple-element.52.refs_0_), channel_id=1, source_target_pairs={{0,16},{8,24},{16,0},{24,8},{1,17},{9,25},{17,1},{25,9},{2,18},{10... | collective-permute-start | bytes 196616 | tf_op jit(solution)/shard_map/ppermute | solution.py:323
  29.7 5.3 %collective-permute-start.3 = (f32[128,128]{1,0:T(8,128)S(1)}, f32[128,128]{1,0:T(8,128)S(1)}, u32[]{:S(2)}, u32[]{:S(2)}) collective-permute-start(f32[128,128]{1,0:T(8,128)S(1)} %get-tuple-element.52.refs_0_), channel_id=1, source_target_pairs={{0,8},{8,0},{16,24},{24,16},{1,9},{9,1},{17,25},{25,17},{2,10},{10... | collective-permute-start | bytes 196616 | tf_op jit(solution)/shard_map/ppermute | solution.py:323
  31.5 9.7 %collective-permute-start.13 = (f32[256,128]{1,0:T(8,128)S(1)}, f32[256,128]{1,0:T(8,128)S(1)}, u32[]{:S(2)}, u32[]{:S(2)}) collective-permute-start(f32[256,128]{1,0:T(8,128)S(1)} %get-tuple-element.47), channel_id=1, source_target_pairs={{0,4},{2,6},{4,0},{6,2},{1,5},{3,7},{5,1},{7,3},{8,12},{10,14},{12... | collective-permute-start | bytes 393224 | tf_op jit(solution)/shard_map/ppermute | solution.py:323
  33.2 8.1 %collective-permute-start.14 = (f32[256,128]{1,0:T(8,128)S(1)}, f32[256,128]{1,0:T(8,128)S(1)}, u32[]{:S(2)}, u32[]{:S(2)}) collective-permute-start(f32[256,128]{1,0:T(8,128)S(1)} %get-tuple-element.48), channel_id=1, source_target_pairs={{0,6},{2,4},{4,2},{6,0},{1,7},{3,5},{5,3},{7,1},{8,14},{10,12},{12... | collective-permute-start | bytes 393224 | tf_op jit(solution)/shard_map/ppermute | solution.py:323
  36.9 5.3 %collective-permute-start.6 = (f32[256,128]{1,0:T(8,128)S(1)}, f32[256,128]{1,0:T(8,128)S(1)}, u32[]{:S(2)}, u32[]{:S(2)}) collective-permute-start(f32[256,128]{1,0:T(8,128)S(1)} %get-tuple-element.40), channel_id=1, source_target_pairs={{0,2},{2,0},{4,6},{6,4},{1,3},{3,1},{5,7},{7,5},{8,10},{10,8},{12,... | collective-permute-start | bytes 393224 | tf_op jit(solution)/shard_map/ppermute | solution.py:323
  38.1 5.2 %collective-permute-start.7 = (f32[256,128]{1,0:T(8,128)S(1)}, f32[256,128]{1,0:T(8,128)S(1)}, u32[]{:S(2)}, u32[]{:S(2)}) collective-permute-start(f32[256,128]{1,0:T(8,128)S(1)} %get-tuple-element.41), channel_id=1, source_target_pairs={{0,4},{2,6},{4,0},{6,2},{1,5},{3,7},{5,1},{7,3},{8,12},{10,14},{12... | collective-permute-start | bytes 393224 | tf_op jit(solution)/shard_map/ppermute | solution.py:323
  39.0 5.9 %collective-permute-start.8 = (f32[256,128]{1,0:T(8,128)S(1)}, f32[256,128]{1,0:T(8,128)S(1)}, u32[]{:S(2)}, u32[]{:S(2)}) collective-permute-start(f32[256,128]{1,0:T(8,128)S(1)} %get-tuple-element.42), channel_id=1, source_target_pairs={{0,6},{2,4},{4,2},{6,0},{1,7},{3,5},{5,3},{7,1},{8,14},{10,12},{12... | collective-permute-start | bytes 393224 | tf_op jit(solution)/shard_map/ppermute | solution.py:323
  45.5 1.6 %collective-permute-start.15 = (f32[128,512]{1,0:T(8,128)S(1)}, f32[128,512]{1,0:T(8,128)S(1)}, u32[]{:S(2)}, u32[]{:S(2)}) collective-permute-start(f32[128,512]{1,0:T(8,128)S(1)} %shard_map.47), channel_id=1, source_target_pairs={{0,1},{1,0},{2,3},{3,2},{4,5},{5,4},{6,7},{7,6},{8,9},{9,8},{10,11... | collective-permute-start | bytes 786440 | tf_op jit(solution)/shard_map/ppermute | solution.py:323

commit v2 on v1

--- a/solution.py
+++ b/solution.py
@@ -113,9 +113,18 @@
     share = BAND // n_col
     per = share // STEP
     for j in range(0, cols, LANES):
+        n = n0 + j + lax.broadcasted_iota(I32, (BAND // STEP, LANES), 1)
+        row = lax.broadcasted_iota(I32, (BAND // STEP, LANES), 0)
+        v = (me ^ (row // per)) * share + (row % per) * STEP
+        c, s = circle((v * n) & (HOLO - 1), HOLO)
+        a_re[:, j : j + LANES] = c
+        a_im[:, j : j + LANES] = -s
+    get.wait()
+    offset = offs[0, 1]
+    for j in range(0, cols, LANES):
         n = n0 + j + lax.broadcasted_iota(I32, (STEP, LANES), 1)
         low = lax.broadcasted_iota(I32, (STEP, LANES), 0)
-        c, s = circle((low * n) & (HOLO - 1), HOLO)
+        c, s = circle((((offset + low) & (HOLO - 1)) * n) & (HOLO - 1), HOLO)
         b_re[:, j : j + LANES] = c
         b_im[:, j : j + LANES] = -s
     for i in range(pieces):
@@ -125,15 +134,6 @@
                 c, s = radians(ph[at : at + STEP, j : j + LANES])
                 field[at : at + STEP, j : j + LANES] = c.astype(BF16)
                 field[rows + at : rows + at + STEP, j : j + LANES] = s.astype(BF16)
-    get.wait()
-    offset = offs[0, 1]
-    for j in range(0, cols, LANES):
-        n = n0 + j + lax.broadcasted_iota(I32, (BAND // STEP, LANES), 1)
-        row = lax.broadcasted_iota(I32, (BAND // STEP, LANES), 0)
-        v = (me ^ (row // per)) * share + (row % per) * STEP
-        c, s = circle((((offset + v) & (HOLO - 1)) * n) & (HOLO - 1), HOLO)
-        a_re[:, j : j + LANES] = c
-        a_im[:, j : j + LANES] = -s
     multiply_band(n_col, n_col - 1, table, field, a_re, a_im, b_re, b_im, out)
 
 
@@ -240,14 +240,28 @@
                 g_lo[at + part : at + part + STEP, :BAND] = -lo
 
 
+def turn_and_send(n_row, n_col, depths, chunk, t, lens_hi, lens_lo, ev, w2, out):
+    part = BAND // (n_col * CHUNKS)
+    both = 2 * part
+    xs = BAND // (n_row * n_col)
+    block = depths * xs
+    at = t * block
+    z = mm(lens_hi[at : at + block, :], w2[...], nt=True)
+    z = z[:, :both] + (z[:, both:] + mm(lens_lo[at : at + block, :], w2[:both, :], nt=True))
+    for d in range(depths):
+        piece = z[d * xs : (d + 1) * xs, :]
+        row = 2 * (chunk * depths + d)
+        turned = piece * ev[row : row + 1, :] + pltpu.roll(piece, part, 1) * ev[row + 1 : row + 2, :]
+        out[d * xs : (d + 1) * xs, :] = turned
+
+
 def lens_kernel(n_row, n_col, depths, chunk, *refs):
     halves = refs[:n_row]
     fl_hi, fl_lo, lens_hi, lens_lo, ev = refs[n_row : n_row + 5]
-    outs = refs[n_row + 5 : n_row + 5 + n_col]
-    x2, w2 = refs[n_row + 5 + n_col :]
+    outs = refs[n_row + 5 : n_row + 4 + n_col]
+    w2, x2 = refs[n_row + 4 + n_col :]
     part = BAND // (n_col * CHUNKS)
     both = 2 * part
-    xs = BAND // (n_row * n_col)
     rows_here = halves[0].shape[1]
     for i, h in enumerate(halves):
         hi, lo = split(h[...])
@@ -267,30 +281,25 @@
     w2[:part, BAND:] = -hi
     w2[both + part :, :BAND] = lo
     w2[both : both + part, BAND:] = -lo
-    block = depths * xs
-    for t in list(range(1, n_col)) + [0]:
-        at = t * block
-        z = mm(lens_hi[at : at + block, :], w2[...], nt=True)
-        z = z[:, :both] + (z[:, both:] + mm(lens_lo[at : at + block, :], w2[:both, :], nt=True))
-        for d in range(depths):
-            piece = z[d * xs : (d + 1) * xs, :]
-            row = 2 * (chunk * depths + d)
-            turned = piece * ev[row : row + 1, :] + pltpu.roll(piece, part, 1) * ev[row + 1 : row + 2, :]
-            outs[t][d * xs : (d + 1) * xs, :] = turned
-
-
-def image_sum(blocks, g_hi, g_lo, lo_rows, hi_rows):
-    x = jnp.concatenate([b[lo_rows:hi_rows, :] for b in blocks], axis=1)
-    hi, lo = split(x)
+    for t in range(n_col - 1, 0, -1):
+        turn_and_send(n_row, n_col, depths, chunk, t, lens_hi, lens_lo, ev, w2, outs[t - 1])
+
+
+def own_lens_kernel(n_row, n_col, depths, chunk, *refs):
+    turn_and_send(n_row, n_col, depths, chunk, 0, *refs)
+
+
+def image_sum(blocks, g_hi, g_lo):
+    hi, lo = split(jnp.concatenate(blocks, axis=1))
     return mm(hi, g_hi[...]) + (mm(lo, g_hi[...]) + mm(hi, g_lo[...]))
 
 
 def image_kernel(n_col, *refs):
-    refs[-1][...] = image_sum(refs[:n_col], refs[n_col], refs[n_col + 1], 0, refs[0].shape[0])
+    refs[-1][...] = image_sum([x[...] for x in refs[:n_col]], refs[n_col], refs[n_col + 1])
 
 
 def power_kernel(n_col, lo_rows, hi_rows, *refs):
-    z = image_sum(refs[:n_col], refs[n_col], refs[n_col + 1], lo_rows, hi_rows)
+    z = image_sum([x[lo_rows:hi_rows, :] for x in refs[:n_col]], refs[n_col], refs[n_col + 1])
     for more in refs[n_col + 2 : -1]:
         z = z + more[lo_rows:hi_rows, :]
     re = z[:, :BAND]
@@ -334,7 +343,6 @@
     block = depths * xs
     spacing = HOLO // (rows * n_row)
     dma = pltpu.SemaphoreType.DMA
-    away = range(n_col - 1, 0, -1)
 
     piece = spec((2 * share, rows))
     table = pltpu.VMEM((2 * share, cols), BF16)
@@ -377,18 +385,19 @@
         for x in got[:-1]:
             half = half + x[2 * h * part : 2 * (h + 1) * part]
         halves = [half] + [swap(half, "row", t) for t in range(1, n_row)]
-        lens = call(
+        piece = spec((block, 2 * part))
+        *lens, w2 = call(
             functools.partial(lens_kernel, n_row, n_col, depths, h),
-            [spec((block, 2 * part))] * n_col,
+            [piece] * (n_col - 1) + [spec((4 * part, 2 * BAND), BF16)],
             n_row + 5,
-            [pltpu.VMEM((4 * part, n_row * rows), BF16), pltpu.VMEM((4 * part, 2 * BAND), BF16)],
+            [pltpu.VMEM((4 * part, n_row * rows), BF16)],
         )(*halves, *tables)
-        blocks.append([lens[0]] + [swap(lens[t], "col", t) for t in away][::-1])
+        own_lens = call(functools.partial(own_lens_kernel, n_row, n_col, depths, h), [piece], 4)(*tables[2:], w2)
+        arrived = [swap(lens[t - 1], "col", t) for t in range(n_col - 1, 0, -1)]
+        blocks.append(list(own_lens) + arrived[::-1])
     for h in range(CHUNKS - 1):
-        sums.append(
-            call(functools.partial(image_kernel, n_col), [spec((block, 2 * BAND))], n_col + 2)(
-                *blocks[h], *image_tables[2 * h : 2 * h + 2]
-            )[0]
+        sums += call(functools.partial(image_kernel, n_col), [spec((block, 2 * BAND))], n_col + 2)(
+            *blocks[h], *image_tables[2 * h : 2 * h + 2]
         )
     size = block // n_pupil
     power = {}
@@ -398,9 +407,10 @@
             [spec((size, BAND))],
             n_col + 2 + len(sums),
         )(*blocks[-1], *image_tables[-2:], *sums)[0]
+    received = [swap(power[t], "pupil", t) for t in range(1, n_pupil)]
     total = power[0]
-    for t in range(1, n_pupil):
-        total = total + swap(power[t], "pupil", t)
+    for x in received:
+        total = total + x
     total = total * (1.0 / (band_offsets.shape[0] * n_pupil))
     return total.reshape(own, xs, BAND)
 

time: 48 us -> 48.1 us (level)
  starting transfers between devices: 21.5 us -> 20.6 us
  waiting for transfers between devices: 11 us -> 11.8 us
    ppermute x16, starting transfers between devices: 21.5 us -> 20.6 us  [swap(): return lax.ppermute(x, axis, [(i, i ^ t) for i in range(n)])]
    ppermute x16, waiting for transfers between devices: 11 us -> 11.8 us  [swap(): return lax.ppermute(x, axis, [(i, i ^ t) for i in range(n)])]
    pallas_call x2 -> x4, Pallas kernels: 3.8 us -> 4.34 us  [the longest x2 3.28 us: local(): call(functools.partial(lens_kernel, n_row, n_col, depths, h), [piece] * (...]
  transfers between devices with their start and end apart: 16 -> 16, of which waited for: 9 -> 8; matrix products, arithmetic and copies ran while one was open for 0% -> 0% of each run, Pallas kernels for 18% -> 19%
where the time goes in v2:
time: 48.1 us; the launch traced here: 48 us
  starting transfers between devices  20.6 us (43%)
  Pallas kernels  14.6 us (30%)
  waiting for transfers between devices  11.8 us (25%)
  other arithmetic  0.77 us (2%)
    ppermute x16, starting transfers between devices, swap(): return lax.ppermute(x, axis, [(i, i ^ t) for i in range(n)])  20.6 us
    ppermute x16, waiting for transfers between devices, swap(): return lax.ppermute(x, axis, [(i, i ^ t) for i in range(n)])  11.8 us
    pallas_call x1, Pallas kernels, local(): tables = lens_tables(offs, in_hbm(depth_codes))  3.31 us
    pallas_call x2, Pallas kernels, local(): call(functools.partial(lens_kernel, n_row, n_col, depths, h), [piece] * (...  3.28 us
    pallas_call x1, Pallas kernels, local(): call(functools.partial(first_kernel, n_col), [piece, spec((2 * rows, cols...  2.57 us
    pallas_call x3, Pallas kernels, local(): call(functools.partial(later_kernel, n_col, t), [piece], 5, [table])  1.53 us
    pallas_call x2, Pallas kernels, local(): call(functools.partial(power_kernel, n_col, t * size, (t + 1) * size), [s...  1.18 us
    pallas_call x2, Pallas kernels, local(): call(functools.partial(own_lens_kernel, n_row, n_col, depths, h), [piece]...  1.05 us
  transfers between devices with their start and end apart: 16, of which 8 were waited for; matrix products, arithmetic and copies ran while one was open for 0% of the time, Pallas kernels for 19%

profile of v2, /device:TPU:0, one launch (start us, length us, event | category | flops | bytes accessed | tf_op | source)
XLA Modules:
  0.0 48.0 jit_solution(3440048292549040694)
XLA Ops:
  0.0 2.6 %shard_map.38 = (f32[256,128]{1,0:T(8,128)S(1)}, bf16[256,2048]{1,0:T(8,128)(2,1)S(1)}, f32[32,2048]{1,0:T(8,128)S(1)}, f32[32,2048]{1,0:T(8,128)S(1)}, f32[16,2048]{1,0:T(8,128)S(1)}, /*index=5*/f32[16,2048]{1,0:T(8,128)S(1)}) custom-call(s32[1,2]{1,0:T(1,128)} %offs_hbm.3, f32[128,2048]{1,0:T(8,128)} %ph_hbm.1), custom_call_target="tpu_custom_call" | custom-call | tf_op jit(solution)/shard_map/pallas_call | solution.py:350
  2.6 0.5 %shard_map.40 = f32[256,128]{1,0:T(8,128)S(1)} custom-call(bf16[256,2048]{1,0:T(8,128)(2,1)S(1)} %get-tuple-element.31.field, f32[32,2048]{1,0:T(8,128)S(1)} %get-tuple-element.32.a_re, f32[32,2048]{1,0:T(8,128)S(1)} %get-tuple-element.33.a_im, f32[16,2048]{1,0:T(8,128)S(1)} %get-tuple-element.34.b_re, f32[16,2048]{1,0:T(8,128)S(1)} %get-tuple-element.35.b_im), custom_call_target="tpu_custom_call" | custom-call | tf_op jit(solution)/shard_map/pallas_call | solution.py:359
  3.1 3.1 %collective-permute-start.1 = (f32[256,128]{1,0:T(8,128)S(1)}, f32[256,128]{1,0:T(8,128)S(1)}, u32[]{:S(2)}, u32[]{:S(2)}) collective-permute-start(f32[256,128]{1,0:T(8,128)S(1)} %shard_map.40), channel_id=1, source_target_pairs={{0,4},{2,6},{4,0},{6,2},{1,5},{3,7},{5,1},{7,3},{8,12},{10,14},{12... | collective-permute-start | bytes 393224 | tf_op jit(solution)/shard_map/ppermute | solution.py:332
  6.2 0.5 %shard_map.41 = f32[256,128]{1,0:T(8,128)S(1)} custom-call(bf16[256,2048]{1,0:T(8,128)(2,1)S(1)} %get-tuple-element.31.field, f32[32,2048]{1,0:T(8,128)S(1)} %get-tuple-element.32.a_re, f32[32,2048]{1,0:T(8,128)S(1)} %get-tuple-element.33.a_im, f32[16,2048]{1,0:T(8,128)S(1)} %get-tuple-element.34.b_re, f32[16,2048]{1,0:T(8,128)S(1)} %get-tuple-element.35.b_im), custom_call_target="tpu_custom_call" | custom-call | tf_op jit(solution)/shard_map/pallas_call | solution.py:359
  6.7 1.6 %collective-permute-start.2 = (f32[256,128]{1,0:T(8,128)S(1)}, f32[256,128]{1,0:T(8,128)S(1)}, u32[]{:S(2)}, u32[]{:S(2)}) collective-permute-start(f32[256,128]{1,0:T(8,128)S(1)} %shard_map.41), channel_id=1, source_target_pairs={{0,2},{2,0},{4,6},{6,4},{1,3},{3,1},{5,7},{7,5},{8,10},{10,8},{12,... | collective-permute-start | bytes 393224 | tf_op jit(solution)/shard_map/ppermute | solution.py:332
  8.2 0.0 collective-permute-start
  8.2 0.5 %shard_map.39 = f32[256,128]{1,0:T(8,128)S(1)} custom-call(bf16[256,2048]{1,0:T(8,128)(2,1)S(1)} %get-tuple-element.31.field, f32[32,2048]{1,0:T(8,128)S(1)} %get-tuple-element.32.a_re, f32[32,2048]{1,0:T(8,128)S(1)} %get-tuple-element.33.a_im, f32[16,2048]{1,0:T(8,128)S(1)} %get-tuple-element.34.b_re, f32[16,2048]{1,0:T(8,128)S(1)} %get-tuple-element.35.b_im), custom_call_target="tpu_custom_call" | custom-call | tf_op jit(solution)/shard_map/pallas_call | solution.py:359
  8.8 0.9 %collective-permute-done.1 = f32[256,128]{1,0:T(8,128)S(1)} collective-permute-done((f32[256,128]{1,0:T(8,128)S(1)}, f32[256,128]{1,0:T(8,128)S(1)}, u32[]{:S(2)}, u32[]{:S(2)}) %collective-permute-start.1) | collective-permute-done | bytes 131104 | tf_op jit(solution)/shard_map/ppermute | solution.py:332
  9.7 3.4 %collective-permute-done.2 = f32[256,128]{1,0:T(8,128)S(1)} collective-permute-done((f32[256,128]{1,0:T(8,128)S(1)}, f32[256,128]{1,0:T(8,128)S(1)}, u32[]{:S(2)}, u32[]{:S(2)}) %collective-permute-start.2) | collective-permute-done | bytes 131104 | tf_op jit(solution)/shard_map/ppermute | solution.py:332
  13.1 1.1 %collective-permute-done = f32[256,128]{1,0:T(8,128)S(1)} collective-permute-done((f32[256,128]{1,0:T(8,128)S(1)}, f32[256,128]{1,0:T(8,128)S(1)}, u32[]{:S(2)}, u32[]{:S(2)}) %collective-permute-start) | collective-permute-done | bytes 131104 | tf_op jit(solution)/shard_map/ppermute | solution.py:332
  14.3 2.9 %collective-permute-start.10 = (f32[128,128]{1,0:T(8,128)S(1)}, f32[128,128]{1,0:T(8,128)S(1)}, u32[]{:S(2)}, u32[]{:S(2)}) collective-permute-start(f32[128,128]{1,0:T(8,128)S(1)} %get-tuple-element.51.refs_0_), channel_id=1, source_target_pairs={{0,16},{8,24},{16,0},{24,8},{1,17},{9,25},{17,1},{25,9},{2,18},{10... | collective-permute-start | bytes 196616 | tf_op jit(solution)/shard_map/ppermute | solution.py:332
  17.1 1.3 %collective-permute-start.11 = (f32[128,128]{1,0:T(8,128)S(1)}, f32[128,128]{1,0:T(8,128)S(1)}, u32[]{:S(2)}, u32[]{:S(2)}) collective-permute-start(f32[128,128]{1,0:T(8,128)S(1)} %get-tuple-element.51.refs_0_), channel_id=1, source_target_pairs={{0,24},{8,16},{16,8},{24,0},{1,25},{9,17},{17,9},{25,1},{2,26},{10... | collective-permute-start | bytes 196616 | tf_op jit(solution)/shard_map/ppermute | solution.py:332
  18.5 0.2 collective-permute-start.9
  18.7 3.3 %shard_map.37 = (bf16[512,1024]{1,0:T(8,128)(2,1)S(1)}, bf16[512,1024]{1,0:T(8,128)(2,1)S(1)}, bf16[1024,1024]{1,0:T(8,128)(2,1)S(1)}, bf16[1024,1024]{1,0:T(8,128)(2,1)S(1)}, f32[32,128]{1,0:T(8,128)S(1)}) custom-call(s32[1,2]{1,0:T(1,128)} %offs_hbm.3, s32[8]{0:T(128)} %codes_hbm.1), custom_call_target="tpu_custom_call" | custom-call | tf_op jit(solution)/shard_map/pallas_call | solution.py:373
  22.0 0.0 collective-permute-done.10.refs_2_
  22.0 1.3 %collective-permute-done.11.refs_3_ = f32[128,128]{1,0:T(8,128)S(1)} collective-permute-done((f32[128,128]{1,0:T(8,128)S(1)}, f32[128,128]{1,0:T(8,128)S(1)}, u32[]{:S(2)}, u32[]{:S(2)}) %collective-permute-start.11) | collective-permute-done | bytes 65568 | tf_op jit(solution)/shard_map/ppermute | solution.py:332
  23.3 0.1 collective-permute-done.9.refs_1_
  23.5 1.6 %shard_map.45 = (f32[256,128]{1,0:T(8,128)S(1)}, f32[256,128]{1,0:T(8,128)S(1)}, f32[256,128]{1,0:T(8,128)S(1)}, bf16[256,1024]{1,0:T(8,128)(2,1)S(1)}) custom-call(f32[128,128]{1,0:T(8,128)S(1)} %get-tuple-element.51.refs_0_, f32[128,128]{1,0:T(8,128)S(1)} %collective-permute-done.9.refs_1_, f32[128,128]{1,0:T(8,128)S(1)} %collective-permute-done.10.refs_2_, ...), custom_call_target="tpu_custom_call" | custom-call | tf_op jit(solution)/shard_map/pallas_call | solution.py:389
  25.1 1.6 %collective-permute-start.12 = (f32[256,128]{1,0:T(8,128)S(1)}, f32[256,128]{1,0:T(8,128)S(1)}, u32[]{:S(2)}, u32[]{:S(2)}) collective-permute-start(f32[256,128]{1,0:T(8,128)S(1)} %get-tuple-element.46), channel_id=1, source_target_pairs={{0,2},{2,0},{4,6},{6,4},{1,3},{3,1},{5,7},{7,5},{8,10},{10,8},{12,... | collective-permute-start | bytes 393224 | tf_op jit(solution)/shard_map/ppermute | solution.py:332
  26.7 0.4 collective-permute-start.3
  27.1 2.2 %collective-permute-start.4 = (f32[128,128]{1,0:T(8,128)S(1)}, f32[128,128]{1,0:T(8,128)S(1)}, u32[]{:S(2)}, u32[]{:S(2)}) collective-permute-start(f32[128,128]{1,0:T(8,128)S(1)} %get-tuple-element.52.refs_0_), channel_id=1, source_target_pairs={{0,16},{8,24},{16,0},{24,8},{1,17},{9,25},{17,1},{25,9},{2,18},{10... | collective-permute-start | bytes 196616 | tf_op jit(solution)/shard_map/ppermute | solution.py:332
  29.3 1.7 %collective-permute-start.5 = (f32[128,128]{1,0:T(8,128)S(1)}, f32[128,128]{1,0:T(8,128)S(1)}, u32[]{:S(2)}, u32[]{:S(2)}) collective-permute-start(f32[128,128]{1,0:T(8,128)S(1)} %get-tuple-element.52.refs_0_), channel_id=1, source_target_pairs={{0,24},{8,16},{16,8},{24,0},{1,25},{9,17},{17,9},{25,1},{2,26},{10... | collective-permute-start | bytes 196616 | tf_op jit(solution)/shard_map/ppermute | solution.py:332
  31.0 1.5 %collective-permute-start.13 = (f32[256,128]{1,0:T(8,128)S(1)}, f32[256,128]{1,0:T(8,128)S(1)}, u32[]{:S(2)}, u32[]{:S(2)}) collective-permute-start(f32[256,128]{1,0:T(8,128)S(1)} %get-tuple-element.47), channel_id=1, source_target_pairs={{0,4},{2,6},{4,0},{6,2},{1,5},{3,7},{5,1},{7,3},{8,12},{10,14},{12... | collective-permute-start | bytes 393224 | tf_op jit(solution)/shard_map/ppermute | solution.py:332
  32.6 0.0 collective-permute-done.3.refs_1_
  32.6 0.5 %collective-permute-start.14 = (f32[256,128]{1,0:T(8,128)S(1)}, f32[256,128]{1,0:T(8,128)S(1)}, u32[]{:S(2)}, u32[]{:S(2)}) collective-permute-start(f32[256,128]{1,0:T(8,128)S(1)} %get-tuple-element.48), channel_id=1, source_target_pairs={{0,6},{2,4},{4,2},{6,0},{1,7},{3,5},{5,3},{7,1},{8,14},{10,12},{12... | collective-permute-start | bytes 393224 | tf_op jit(solution)/shard_map/ppermute | solution.py:332
  33.1 0.0 collective-permute-done.4.refs_2_
  33.1 2.3 %collective-permute-done.5.refs_3_ = f32[128,128]{1,0:T(8,128)S(1)} collective-permute-done((f32[128,128]{1,0:T(8,128)S(1)}, f32[128,128]{1,0:T(8,128)S(1)}, u32[]{:S(2)}, u32[]{:S(2)}) %collective-permute-start.5) | collective-permute-done | bytes 65568 | tf_op jit(solution)/shard_map/ppermute | solution.py:332
  35.4 1.6 %shard_map.42 = (f32[256,128]{1,0:T(8,128)S(1)}, f32[256,128]{1,0:T(8,128)S(1)}, f32[256,128]{1,0:T(8,128)S(1)}, bf16[256,1024]{1,0:T(8,128)(2,1)S(1)}) custom-call(f32[128,128]{1,0:T(8,128)S(1)} %get-tuple-element.52.refs_0_, f32[128,128]{1,0:T(8,128)S(1)} %collective-permute-done.3.refs_1_, f32[128,128]{1,0:T(8,128)S(1)} %collective-permute-done.4.refs_2_, ...), custom_call_target="tpu_custom_call" | custom-call | tf_op jit(solution)/shard_map/pallas_call | solution.py:389
  37.0 0.8 %collective-permute-start.6 = (f32[256,128]{1,0:T(8,128)S(1)}, f32[256,128]{1,0:T(8,128)S(1)}, u32[]{:S(2)}, u32[]{:S(2)}) collective-permute-start(f32[256,128]{1,0:T(8,128)S(1)} %get-tuple-element.40), channel_id=1, source_target_pairs={{0,2},{2,0},{4,6},{6,4},{1,3},{3,1},{5,7},{7,5},{8,10},{10,8},{12,... | collective-permute-start | bytes 393224 | tf_op jit(solution)/shard_map/ppermute | solution.py:332
  37.8 1.4 %collective-permute-start.7 = (f32[256,128]{1,0:T(8,128)S(1)}, f32[256,128]{1,0:T(8,128)S(1)}, u32[]{:S(2)}, u32[]{:S(2)}) collective-permute-start(f32[256,128]{1,0:T(8,128)S(1)} %get-tuple-element.41), channel_id=1, source_target_pairs={{0,4},{2,6},{4,0},{6,2},{1,5},{3,7},{5,1},{7,3},{8,12},{10,14},{12... | collective-permute-start | bytes 393224 | tf_op jit(solution)/shard_map/ppermute | solution.py:332
  39.1 0.0 collective-permute-done.12.refs_1_
  39.2 1.4 %collective-permute-start.8 = (f32[256,128]{1,0:T(8,128)S(1)}, f32[256,128]{1,0:T(8,128)S(1)}, u32[]{:S(2)}, u32[]{:S(2)}) collective-permute-start(f32[256,128]{1,0:T(8,128)S(1)} %get-tuple-element.42), channel_id=1, source_target_pairs={{0,6},{2,4},{4,2},{6,0},{1,7},{3,5},{5,3},{7,1},{8,14},{10,12},{12... | collective-permute-start | bytes 393224 | tf_op jit(solution)/shard_map/ppermute | solution.py:332
  40.6 0.7 %shard_map.44 = (bf16[512,1024]{1,0:T(8,128)(2,1)S(1)}, bf16[512,1024]{1,0:T(8,128)(2,1)S(1)}, bf16[512,1024]{1,0:T(8,128)(2,1)S(1)}, bf16[512,1024]{1,0:T(8,128)(2,1)S(1)}) custom-call(), custom_call_target="tpu_custom_call" | custom-call | tf_op jit(solution)/shard_map/pallas_call | solution.py:374
  41.3 0.5 %shard_map.46.refs_0_ = f32[256,128]{1,0:T(8,128)S(1)} custom-call(bf16[1024,1024]{1,0:T(8,128)(2,1)S(1)} %get-tuple-element.28.refs_6_.refs_0_, bf16[1024,1024]{1,0:T(8,128)(2,1)S(1)} %get-tuple-element.29.refs_7_.refs_1_, f32[32,128]{1,0:T(8,128)S(1)} %get-tuple-element.30.refs_8_.refs_2_, bf16[256,1024]{1,0:T(8,128)(2,1)S(1)} %get-tuple-element.45.refs_3_), custom_call_target="tpu_custom_call" | custom-call | tf_op jit(solution)/shard_map/pallas_call | solution.py:395
  41.8 0.5 %shard_map.43.refs_0_ = f32[256,128]{1,0:T(8,128)S(1)} custom-call(bf16[1024,1024]{1,0:T(8,128)(2,1)S(1)} %get-tuple-element.28.refs_6_.refs_0_, bf16[1024,1024]{1,0:T(8,128)(2,1)S(1)} %get-tuple-element.29.refs_7_.refs_1_, f32[32,128]{1,0:T(8,128)S(1)} %get-tuple-element.30.refs_8_.refs_2_, bf16[256,1024]{1,0:T(8,128)(2,1)S(1)} %get-tuple-element.39.refs_3_), custom_call_target="tpu_custom_call" | custom-call | tf_op jit(solution)/shard_map/pallas_call | solution.py:395
  42.4 0.0 collective-permute-done.13.refs_2_
  42.4 0.0 collective-permute-done.14.refs_3_
  42.4 1.0 %shard_map.47.refs_6_ = f32[256,1024]{1,0:T(8,128)S(1)} custom-call(f32[256,128]{1,0:T(8,128)S(1)} %shard_map.46.refs_0_, f32[256,128]{1,0:T(8,128)S(1)} %collective-permute-done.12.refs_1_, f32[256,128]{1,0:T(8,128)S(1)} %collective-permute-done.13.refs_2_, f32[256,128]{1,0:T(8,128)S(1)} %collective-permute-done.14.refs_3_, ...), custom_call_target="tpu_custom_call" | custom-call | tf_op jit(solution)/shard_map/pallas_call | solution.py:399
  43.4 0.0 collective-permute-done.6.refs_1_
  43.4 0.0 collective-permute-done.7.refs_2_
  43.4 1.6 %collective-permute-done.8.refs_3_ = f32[256,128]{1,0:T(8,128)S(1)} collective-permute-done((f32[256,128]{1,0:T(8,128)S(1)}, f32[256,128]{1,0:T(8,128)S(1)}, u32[]{:S(2)}, u32[]{:S(2)}) %collective-permute-start.8) | collective-permute-done | bytes 131104 | tf_op jit(solution)/shard_map/ppermute | solution.py:332
  45.0 0.6 %shard_map.49 = f32[128,512]{1,0:T(8,128)S(1)} custom-call(f32[256,128]{1,0:T(8,128)S(1)} %shard_map.43.refs_0_, f32[256,128]{1,0:T(8,128)S(1)} %collective-permute-done.6.refs_1_, f32[256,128]{1,0:T(8,128)S(1)} %collective-permute-done.7.refs_2_, f32[256,128]{1,0:T(8,128)S(1)} %collective-permute-done.8.refs_3_, ...), custom_call_target="tpu_custom_call" | custom-call | tf_op jit(solution)/shard_map/pallas_call | solution.py:405
  45.6 0.1 collective-permute-start.15
  45.7 0.6 %shard_map.48 = f32[128,512]{1,0:T(8,128)S(1)} custom-call(f32[256,128]{1,0:T(8,128)S(1)} %shard_map.43.refs_0_, f32[256,128]{1,0:T(8,128)S(1)} %collective-permute-done.6.refs_1_, f32[256,128]{1,0:T(8,128)S(1)} %collective-permute-done.7.refs_2_, f32[256,128]{1,0:T(8,128)S(1)} %collective-permute-done.8.refs_3_, ...), custom_call_target="tpu_custom_call" | custom-call | tf_op jit(solution)/shard_map/pallas_call | solution.py:405
  46.3 0.9 %collective-permute-done.15 = f32[128,512]{1,0:T(8,128)S(1)} collective-permute-done((f32[128,512]{1,0:T(8,128)S(1)}, f32[128,512]{1,0:T(8,128)S(1)}, u32[]{:S(2)}, u32[]{:S(2)}) %collective-permute-start.15) | collective-permute-done | bytes 262176 | tf_op jit(solution)/shard_map/ppermute | solution.py:332
  47.2 0.7 %add_multiply_fusion = f32[128,512]{1,0:T(8,128)} fusion(f32[128,512]{1,0:T(8,128)S(1)} %shard_map.48, f32[128,512]{1,0:T(8,128)S(1)} %collective-permute-done.15), kind=kLoop, calls=%fused_computation | loop fusion | flops 131072 | bytes 786432 | tf_op jit(solution)/shard_map/mul | solution.py:414
  (1 shorter events, 0.0 us)
Async XLA Ops:
  3.1 6.6 %collective-permute-start.1 = (f32[256,128]{1,0:T(8,128)S(1)}, f32[256,128]{1,0:T(8,128)S(1)}, u32[]{:S(2)}, u32[]{:S(2)}) collective-permute-start(f32[256,128]{1,0:T(8,128)S(1)} %shard_map.40), channel_id=1, source_target_pairs={{0,4},{2,6},{4,0},{6,2},{1,5},{3,7},{5,1},{7,3},{8,12},{10,14},{12... | collective-permute-start | bytes 393224 | tf_op jit(solution)/shard_map/ppermute | solution.py:332
  6.7 6.4 %collective-permute-start.2 = (f32[256,128]{1,0:T(8,128)S(1)}, f32[256,128]{1,0:T(8,128)S(1)}, u32[]{:S(2)}, u32[]{:S(2)}) collective-permute-start(f32[256,128]{1,0:T(8,128)S(1)} %shard_map.41), channel_id=1, source_target_pairs={{0,2},{2,0},{4,6},{6,4},{1,3},{3,1},{5,7},{7,5},{8,10},{10,8},{12,... | collective-permute-start | bytes 393224 | tf_op jit(solution)/shard_map/ppermute | solution.py:332
  8.2 6.0 %collective-permute-start = (f32[256,128]{1,0:T(8,128)S(1)}, f32[256,128]{1,0:T(8,128)S(1)}, u32[]{:S(2)}, u32[]{:S(2)}) collective-permute-start(f32[256,128]{1,0:T(8,128)S(1)} %get-tuple-element.36), channel_id=1, source_target_pairs={{0,6},{2,4},{4,2},{6,0},{1,7},{3,5},{5,3},{7,1},{8,14},{10,12},{12... | collective-permute-start | bytes 393224 | tf_op jit(solution)/shard_map/ppermute | solution.py:332
  14.3 7.8 %collective-permute-start.10 = (f32[128,128]{1,0:T(8,128)S(1)}, f32[128,128]{1,0:T(8,128)S(1)}, u32[]{:S(2)}, u32[]{:S(2)}) collective-permute-start(f32[128,128]{1,0:T(8,128)S(1)} %get-tuple-element.51.refs_0_), channel_id=1, source_target_pairs={{0,16},{8,24},{16,0},{24,8},{1,17},{9,25},{17,1},{25,9},{2,18},{10... | collective-permute-start | bytes 196616 | tf_op jit(solution)/shard_map/ppermute | solution.py:332
  17.1 6.2 %collective-permute-start.11 = (f32[128,128]{1,0:T(8,128)S(1)}, f32[128,128]{1,0:T(8,128)S(1)}, u32[]{:S(2)}, u32[]{:S(2)}) collective-permute-start(f32[128,128]{1,0:T(8,128)S(1)} %get-tuple-element.51.refs_0_), channel_id=1, source_target_pairs={{0,24},{8,16},{16,8},{24,0},{1,25},{9,17},{17,9},{25,1},{2,26},{10... | collective-permute-start | bytes 196616 | tf_op jit(solution)/shard_map/ppermute | solution.py:332
  18.5 5.0 %collective-permute-start.9 = (f32[128,128]{1,0:T(8,128)S(1)}, f32[128,128]{1,0:T(8,128)S(1)}, u32[]{:S(2)}, u32[]{:S(2)}) collective-permute-start(f32[128,128]{1,0:T(8,128)S(1)} %get-tuple-element.51.refs_0_), channel_id=1, source_target_pairs={{0,8},{8,0},{16,24},{24,16},{1,9},{9,1},{17,25},{25,17},{2,10},{10... | collective-permute-start | bytes 196616 | tf_op jit(solution)/shard_map/ppermute | solution.py:332
  25.1 14.0 %collective-permute-start.12 = (f32[256,128]{1,0:T(8,128)S(1)}, f32[256,128]{1,0:T(8,128)S(1)}, u32[]{:S(2)}, u32[]{:S(2)}) collective-permute-start(f32[256,128]{1,0:T(8,128)S(1)} %get-tuple-element.46), channel_id=1, source_target_pairs={{0,2},{2,0},{4,6},{6,4},{1,3},{3,1},{5,7},{7,5},{8,10},{10,8},{12,... | collective-permute-start | bytes 393224 | tf_op jit(solution)/shard_map/ppermute | solution.py:332
  26.7 5.9 %collective-permute-start.3 = (f32[128,128]{1,0:T(8,128)S(1)}, f32[128,128]{1,0:T(8,128)S(1)}, u32[]{:S(2)}, u32[]{:S(2)}) collective-permute-start(f32[128,128]{1,0:T(8,128)S(1)} %get-tuple-element.52.refs_0_), channel_id=1, source_target_pairs={{0,8},{8,0},{16,24},{24,16},{1,9},{9,1},{17,25},{25,17},{2,10},{10... | collective-permute-start | bytes 196616 | tf_op jit(solution)/shard_map/ppermute | solution.py:332
  27.1 6.0 %collective-permute-start.4 = (f32[128,128]{1,0:T(8,128)S(1)}, f32[128,128]{1,0:T(8,128)S(1)}, u32[]{:S(2)}, u32[]{:S(2)}) collective-permute-start(f32[128,128]{1,0:T(8,128)S(1)} %get-tuple-element.52.refs_0_), channel_id=1, source_target_pairs={{0,16},{8,24},{16,0},{24,8},{1,17},{9,25},{17,1},{25,9},{2,18},{10... | collective-permute-start | bytes 196616 | tf_op jit(solution)/shard_map/ppermute | solution.py:332
  29.3 6.1 %collective-permute-start.5 = (f32[128,128]{1,0:T(8,128)S(1)}, f32[128,128]{1,0:T(8,128)S(1)}, u32[]{:S(2)}, u32[]{:S(2)}) collective-permute-start(f32[128,128]{1,0:T(8,128)S(1)} %get-tuple-element.52.refs_0_), channel_id=1, source_target_pairs={{0,24},{8,16},{16,8},{24,0},{1,25},{9,17},{17,9},{25,1},{2,26},{10... | collective-permute-start | bytes 196616 | tf_op jit(solution)/shard_map/ppermute | solution.py:332
  31.0 11.3 %collective-permute-start.13 = (f32[256,128]{1,0:T(8,128)S(1)}, f32[256,128]{1,0:T(8,128)S(1)}, u32[]{:S(2)}, u32[]{:S(2)}) collective-permute-start(f32[256,128]{1,0:T(8,128)S(1)} %get-tuple-element.47), channel_id=1, source_target_pairs={{0,4},{2,6},{4,0},{6,2},{1,5},{3,7},{5,1},{7,3},{8,12},{10,14},{12... | collective-permute-start | bytes 393224 | tf_op jit(solution)/shard_map/ppermute | solution.py:332
  32.6 9.8 %collective-permute-start.14 = (f32[256,128]{1,0:T(8,128)S(1)}, f32[256,128]{1,0:T(8,128)S(1)}, u32[]{:S(2)}, u32[]{:S(2)}) collective-permute-start(f32[256,128]{1,0:T(8,128)S(1)} %get-tuple-element.48), channel_id=1, source_target_pairs={{0,6},{2,4},{4,2},{6,0},{1,7},{3,5},{5,3},{7,1},{8,14},{10,12},{12... | collective-permute-start | bytes 393224 | tf_op jit(solution)/shard_map/ppermute | solution.py:332
  37.0 6.4 %collective-permute-start.6 = (f32[256,128]{1,0:T(8,128)S(1)}, f32[256,128]{1,0:T(8,128)S(1)}, u32[]{:S(2)}, u32[]{:S(2)}) collective-permute-start(f32[256,128]{1,0:T(8,128)S(1)} %get-tuple-element.40), channel_id=1, source_target_pairs={{0,2},{2,0},{4,6},{6,4},{1,3},{3,1},{5,7},{7,5},{8,10},{10,8},{12,... | collective-permute-start | bytes 393224 | tf_op jit(solution)/shard_map/ppermute | solution.py:332
  37.8 5.6 %collective-permute-start.7 = (f32[256,128]{1,0:T(8,128)S(1)}, f32[256,128]{1,0:T(8,128)S(1)}, u32[]{:S(2)}, u32[]{:S(2)}) collective-permute-start(f32[256,128]{1,0:T(8,128)S(1)} %get-tuple-element.41), channel_id=1, source_target_pairs={{0,4},{2,6},{4,0},{6,2},{1,5},{3,7},{5,1},{7,3},{8,12},{10,14},{12... | collective-permute-start | bytes 393224 | tf_op jit(solution)/shard_map/ppermute | solution.py:332
  39.2 5.9 %collective-permute-start.8 = (f32[256,128]{1,0:T(8,128)S(1)}, f32[256,128]{1,0:T(8,128)S(1)}, u32[]{:S(2)}, u32[]{:S(2)}) collective-permute-start(f32[256,128]{1,0:T(8,128)S(1)} %get-tuple-element.42), channel_id=1, source_target_pairs={{0,6},{2,4},{4,2},{6,0},{1,7},{3,5},{5,3},{7,1},{8,14},{10,12},{12... | collective-permute-start | bytes 393224 | tf_op jit(solution)/shard_map/ppermute | solution.py:332
  45.6 1.6 %collective-permute-start.15 = (f32[128,512]{1,0:T(8,128)S(1)}, f32[128,512]{1,0:T(8,128)S(1)}, u32[]{:S(2)}, u32[]{:S(2)}) collective-permute-start(f32[128,512]{1,0:T(8,128)S(1)} %shard_map.49), channel_id=1, source_target_pairs={{0,1},{1,0},{2,3},{3,2},{4,5},{5,4},{6,7},{7,6},{8,9},{9,8},{10,11... | collective-permute-start | bytes 786440 | tf_op jit(solution)/shard_map/ppermute | solution.py:332
